TPU v7x, 32 devices: a whole 2x2x4 slice. The times are simulated.
32 devices in a mesh: band: 8 (over z, y), col: 4 (over x, core).
Axes of the slice: x: 2, y: 2, z: 4, core: 2. Of those that a mesh axis runs over, the one named last changes fastest.
Arguments:
- valence_wave: bfloat16 [16, 96, 9216], P('band', 'col'), may hold values from -6 to 6
- conduction_wave: bfloat16 [8, 96, 9216], P('band', 'col'), may hold values from -6 to 6
- valence_index: int32 [16], replicated, may hold values from 0 to 4095
- occupied_energy: float32 [4096], replicated, may hold values from -6 to -0.5
- conduction_energy: float32 [8], replicated, may hold values from 0.5 to 8
- frequency: float32 [4], replicated, may hold values from 0.5 to 16
- gvec_cell: int32 [8192], P('col'), may hold values from 0 to 221183, as said below
- block_cell: int32 [16], P('col'), may hold values from 0 to 221183, as said below
Outputs:
- chi: float32 [8192, 128], P(('col', 'band'))
Inputs may be any that keep to these rules, and one draw needn't show every extreme that they name: `gvec_cell`: for rows j of owner k (k * 2048 <= j < (k + 1) * 2048) the entry is (kx 24 + ky - k * 24) * 96 + kz for the G vector's grid point (kx, ky, kz), whose ky lies in [k * 24, (k + 1) * 24); no point appears twice among the rows and block columns of one owner. `block_cell`: block column m has owner k = m // 4 and is encoded as for gvec_cell; its points differ from every row point of the same owner.
All inputs are finite; a program needn't handle non-finite values.
Results may differ from a plain program's by a relative error of at most 0.018.
Values may be sent and summed in bfloat16 or wider, within the bound.
A program may use at most 192 MiB of HBM per device.

v0:
```python
import math

import jax
import jax.numpy as jnp
from jax import lax
from jax.sharding import PartitionSpec as P

GY = 96


def dft_tables(length, factor, out_type):
    indices = jnp.arange(length, dtype=jnp.int32)
    phases = indices[:, None] * indices[None, :] % length
    angles = phases.astype(jnp.float32) * (2.0 * math.pi / length)
    return (
        (jnp.cos(angles) * factor).astype(out_type),
        (-jnp.sin(angles) * factor).astype(out_type),
    )


def weighted_columns(block, weights):
    columns = block.astype(jnp.float32)
    stacked = jnp.stack([columns, jnp.stack([-columns[1], columns[0]])])
    scaled = stacked[None] * weights[:, None, None, :, None]
    scaled = scaled.transpose(2, 3, 0, 1, 4).astype(jnp.bfloat16)
    return scaled.reshape(2, block.shape[1], -1)


def phase_tables(rows, cols, length, factor, out_type):
    phases = rows[:, None] * cols[None, :] % length
    angles = phases.astype(jnp.float32) * (2.0 * math.pi / length)
    return (
        (jnp.cos(angles) * factor).astype(out_type),
        (-jnp.sin(angles) * factor).astype(out_type),
    )


def one_hot(indices, length):
    span = jnp.arange(length, dtype=jnp.int32)
    return (indices[..., None] == span).astype(jnp.bfloat16)


def per_device(
    valence_wave,
    conduction_wave,
    valence_index,
    occupied_energy,
    conduction_energy,
    frequency,
    gvec_cell,
    block_cell,
):
    local_valence, slab_x, plane_size = valence_wave.shape
    band_count = lax.axis_size("band")
    col_count = lax.axis_size("col")
    both = ("col", "band")
    grid_x = slab_x * col_count
    grid_y = GY
    grid_z = plane_size // grid_y
    slab = grid_y // col_count * grid_z
    total_conduction = conduction_energy.shape[0]
    total_valence = local_valence * band_count
    pairs = local_valence * total_conduction
    lanes = pairs * slab_x
    norm_factor = 1.0 / math.sqrt(total_valence * total_conduction)
    bf16, f32 = jnp.bfloat16, jnp.float32

    conduction_all = lax.all_gather(conduction_wave, "band", axis=0, tiled=True)
    products = (valence_wave.astype(f32)[:, None] * conduction_all.astype(f32)[None]).astype(bf16)
    products = products.reshape(lanes, plane_size).T.reshape(grid_y, grid_z, lanes)

    z_cosine, z_sine = dft_tables(grid_z, 1.0, bf16)
    y_cosine, y_sine = dft_tables(grid_y, 1.0 / math.sqrt(grid_y * grid_z), bf16)
    z_table = jnp.stack([z_cosine, z_sine])
    y_table = jnp.stack([jnp.stack([y_cosine, -y_sine]), jnp.stack([y_sine, y_cosine])])
    z_done = jnp.einsum("rkz,yzn->rkyn", z_table, products, preferred_element_type=f32).astype(bf16)
    planes = jnp.einsum("srjy,rkyn->sjkn", y_table, z_done, preferred_element_type=f32).astype(bf16)
    planes = planes.reshape(2, col_count, slab, lanes)

    lane = jnp.arange(lanes, dtype=jnp.int32)
    plane_of = lax.axis_index("col") * slab_x + lane % slab_x
    x_cosine, x_sine = phase_tables(
        jnp.arange(grid_x, dtype=jnp.int32), plane_of, grid_x, 1.0 / math.sqrt(grid_x), bf16
    )
    x_table = jnp.concatenate([x_cosine, x_sine], axis=1)
    fold = (lane[:, None] // slab_x == jnp.arange(pairs, dtype=jnp.int32)[None, :]).astype(bf16)

    def partial_density(cells):
        picked = jnp.einsum(
            "ogc,socn->sogn", one_hot(cells % slab, slab), planes, preferred_element_type=f32
        ).astype(bf16)
        factors = jnp.einsum(
            "ogk,km->ogm", one_hot(cells // slab, grid_x), x_table, preferred_element_type=f32
        ).astype(bf16)
        cosine = factors[..., :lanes].astype(f32)
        sine = factors[..., lanes:].astype(f32)
        real = picked[0].astype(f32)
        imag = picked[1].astype(f32)
        turned = (
            (cosine * real - sine * imag).astype(bf16),
            (sine * real + cosine * imag).astype(bf16),
        )
        return jnp.stack(
            [jnp.einsum("ogn,np->pog", part, fold, preferred_element_type=f32) for part in turned]
        )

    cells_all = lax.all_gather(gvec_cell, "col", axis=0)
    blocks_all = lax.all_gather(block_cell, "col", axis=0)
    block_part = partial_density(blocks_all).reshape(2, pairs, -1)
    row_part = partial_density(cells_all).astype(bf16).reshape(2, pairs, -1)

    block_parts = lax.all_gather(block_part, both, axis=0).reshape(
        col_count, band_count, 2, pairs, -1
    )
    block = jnp.sum(block_parts, axis=0).astype(bf16)
    block = block.transpose(1, 0, 2, 3).reshape(2, band_count * pairs, -1)
    pieces = row_part.reshape(2, pairs, col_count * band_count, -1).transpose(2, 0, 1, 3)
    received = lax.all_to_all(pieces, both, split_axis=0, concat_axis=0, tiled=True)
    received = received.reshape(col_count, band_count, 2, pairs, -1)
    rows = jnp.sum(received.astype(f32), axis=0).astype(bf16)
    rows = rows.transpose(1, 0, 2, 3).reshape(2, band_count * pairs, -1)

    occupied_range = jnp.arange(occupied_energy.shape[0], dtype=jnp.int32)
    valence_energy = jnp.sum(
        jnp.where(valence_index[:, None] == occupied_range[None, :], occupied_energy[None, :], 0.0),
        axis=1,
    )
    gap = (conduction_energy[None, :] - valence_energy[:, None]).reshape(1, -1)
    freq_column = frequency[:, None]
    weights = -4.0 * gap / (gap * gap + freq_column * freq_column) * norm_factor
    right_side = weighted_columns(block, weights)
    return jnp.einsum("rpg,rpc->gc", rows, right_side, preferred_element_type=jnp.float32)


def solution(mesh):
    return jax.shard_map(
        per_device,
        mesh=mesh,
        in_specs=(
            P("band", "col", None),
            P("band", "col", None),
            P(),
            P(),
            P(),
            P(),
            P("col"),
            P("col"),
        ),
        out_specs=P(("col", "band"), None),
        check_vma=False,
    )
```

profile of v0, /device:TPU:0, one launch (start us, length us, event | category | flops | bytes accessed | tf_op | source)
XLA Modules:
  0.0 293.2 jit_solution(627033684000209197)
XLA Ops:
  6.5 0.0 all-gather.4.cloned.1.call-start
  6.5 0.7 all-gather.4.cloned.1.call-update
  7.3 1.3 convert_element_type.227
  8.6 1.2 dynamic-slice
  10.5 0.9 dynamic-update-slice
  11.3 6.4 %all-reduce = s32[16]{0:T(128)S(1)} all-reduce(s32[16]{0:T(128)S(1)} %dynamic-update-slice), channel_id=3, replica_groups=mesh['band'=8,'col'=4] {'col'}, use_global_device_ids=true, to_apply=%add | all-reduce | flops 16 | bytes 128
  17.7 0.1 reshape.289
  17.8 0.1 reshape.291
  17.9 0.1 reshape.295
  18.0 0.9 select_reduce_fusion
  18.9 0.7 subtract_multiply_fusion.1
  19.6 0.1 mul.298
  19.7 0.1 mul.300
  19.8 0.7 mul.301
  20.6 5.4 %all-gather = s32[8192]{0:T(1024)S(1)} all-gather(s32[2048]{0:T(1024)} %param.14), channel_id=2, replica_groups=mesh['band'=8,'col'=4] {'col'}, dimensions={0}, use_global_device_ids=true | all-gather | bytes 40960 | tf_op jit(solution)/shard_map/all_gather | solution.py:107
  26.1 0.2 fusion.66
  26.3 0.2 multiply_convert_fusion.3
  26.5 0.2 fusion.46
  26.8 0.1 divide_multiply_fusion
  26.9 0.6 multiply_convert_fusion.2
  27.5 0.2 convolution_convert_fusion.3
  27.8 6.5 %convolution_convert_fusion.1 = bf16[4,2048,768]{2,1,0:T(8,128)(2,1)} fusion(s32[4,2048]{1,0:T(4,128)S(1)} %get-tuple-element.7, bf16[96,384]{1,0:T(8,128)(2,1)S(1)} %get-tuple-element.16, bf16[96,384]{1,0:T(8,128)(2,1)S(1)} %get-tuple-element.15), kind=kOutput, calls=%fused_computation.18 | convolution fusion | flops 1215332352 | bytes 12763136 | tf_op jit(solution)/shard_map/ogk,km->ogm/dot_general | solution.py:92
  34.3 42.6 %all-gather.4.cloned.1.call-done = bf16[8,24,9216]{2,1,0:T(8,128)(2,1)} async-done(((bf16[1,24,9216]{2,1,0:T(8,128)(2,1)}), bf16[8,24,9216]{2,1,0:T(8,128)(2,1)}) %all-gather.4.cloned.1.call-update) | async-done | bytes 3538960 | tf_op jit(solution)/shard_map/all_gather | solution.py:68
  76.9 5.7 %convert_element_type.228 = f32[8,24,9216]{2,1,0:T(8,128)} convert(bf16[8,24,9216]{2,1,0:T(8,128)(2,1)} %all-gather.4.cloned.1.call-done) | non-fusion elementwise | flops 1769472 | bytes 10616832 | tf_op jit(solution)/shard_map/convert_element_type | solution.py:69
  82.6 7.1 %multiply_convert_fusion = bf16[2,8,24,9216]{3,2,1,0:T(8,128)(2,1)} fusion(f32[8,24,9216]{2,1,0:T(8,128)} %convert_element_type.228, f32[2,24,9216]{2,1,0:T(8,128)S(1)} %convert_element_type.227), kind=kLoop, calls=%fused_computation.11 | loop fusion | flops 7077888 | bytes 15925248 | tf_op jit(solution)/shard_map/convert_element_type | solution.py:69
  89.7 10.3 %copy.72 = bf16[9216,384]{1,0:T(8,128)(2,1)} copy(bf16[9216,384]{0,1:T(8,128)(2,1)} %bitcast.138) | data formatting | bytes 14155776 | tf_op jit(solution)/shard_map/transpose | solution.py:70
  100.0 10.0 %convolution_convert_fusion = bf16[2,96,96,384]{3,1,2,0:T(8,128)(2,1)} fusion(bf16[96,96,384,1]{2,1,0,3:T(8,128)(2,1)} %bitcast.137, bf16[1,96,96]{2,1,0:T(8,128)(2,1)S(1)} %get-tuple-element.22, bf16[1,96,96]{2,1,0:T(8,128)(2,1)S(1)} %get-tuple-element.21), kind=kOutput, calls=%fused_computation.12 | convolution fusion | flops 1366106112 | bytes 21270528 | tf_op jit(solution)/shard_map/rkz,yzn->rkyn/dot_general | solution.py:76
  110.0 19.0 %bitcast_convert_fusion = bf16[2,96,96,384]{3,1,2,0:T(8,128)(2,1)} fusion(bf16[2,96,96,384]{3,1,2,0:T(8,128)(2,1)} %convolution_convert_fusion, bf16[1,2,96,96]{3,2,1,0:T(8,128)(2,1)S(1)} %get-tuple-element.12, bf16[1,2,96,96]{3,2,1,0:T(8,128)(2,1)S(1)} %get-tuple-element.11), kind=kOutput, calls=%fused_computation.4 | convolution fusion | flops 2725134336 | bytes 28385280 | tf_op jit(solution)/shard_map/srjy,rkyn->sjkn/dot_general | solution.py:77
  129.0 15.2 %copy.74 = bf16[2,96,96,384]{3,2,1,0:T(8,128)(2,1)} copy(bf16[2,96,96,384]{3,1,2,0:T(8,128)(2,1)} %bitcast_convert_fusion) | data formatting | bytes 28311552 | tf_op jit(solution)/shard_map/convert_element_type | solution.py:77
  144.2 35.4 %convert_bitcast_fusion = bf16[2,4,2048,384]{3,2,1,0:T(8,128)(2,1)} fusion(bf16[2,4,2304,384]{3,2,1,0:T(8,128)(2,1)} %bitcast.135, s32[4,2048]{1,0:T(4,128)S(1)} %get-tuple-element.8), kind=kOutput, calls=%fused_computation.17 | convolution fusion | flops 29016195072 | bytes 26771456 | tf_op jit(solution)/shard_map/ogc,socn->sogn/dot_general | solution.py:89
  179.6 0.0 copy-start
  179.6 9.9 %fusion.20 = bf16[16,4,2048]{2,0,1:T(8,128)(2,1)S(1)} fusion(bf16[2,4,2048,384]{3,2,1,0:T(8,128)(2,1)} %convert_bitcast_fusion, bf16[4,2048,768]{2,1,0:T(8,128)(2,1)} %convolution_convert_fusion.1, s32[384]{0:T(512)S(1)} %add_select_fusion.6), kind=kOutput, calls=%fused_computation.28 | convolution fusion | flops 125966336 | bytes 25429504 | tf_op jit(solution)/shard_map/ogn,np->pog/dot_general | solution.py:104
  189.5 2.0 copy-done
  191.5 6.8 %fusion.23 = bf16[16,4,2048]{2,0,1:T(8,128)(2,1)S(1)} fusion(bf16[2,4,2048,384]{3,2,1,0:T(8,128)(2,1)S(1)} %copy-done, bf16[4,2048,768]{2,1,0:T(8,128)(2,1)} %convolution_convert_fusion.1, s32[384]{0:T(512)S(1)} %add_select_fusion.6), kind=kOutput, calls=%fused_computation.29 | convolution fusion | flops 125966336 | bytes 25429504 | tf_op jit(solution)/shard_map/ogn,np->pog/dot_general | solution.py:104
  198.3 7.0 %fusion.27 = bf16[2,4,4,384]{3,2,1,0:T(4,128)(2,1)S(1)} fusion(bf16[2,4,2304,384]{3,2,1,0:T(8,128)(2,1)} %bitcast.136, s32[4,4]{1,0:T(4,128)S(1)} %get-tuple-element.14), kind=kOutput, calls=%fused_computation.34 | convolution fusion | flops 56672256 | bytes 14180416 | tf_op jit(solution)/shard_map/ogc,socn->sogn/dot_general | solution.py:89
  205.3 0.2 copy.77
  205.5 0.2 stack.59
  205.7 0.2 copy.78
  205.9 0.2 stack.60
  206.1 0.1 maximum_bitcast_fusion
  206.2 1.1 copy.79
  207.3 3.3 %all-to-all-start = ((bf16[32,2,16,256]{3,2,1,0:T(8,128)(2,1)}), bf16[32,2,16,256]{3,2,1,0:T(8,128)(2,1)S(1)}, u32[]{:S(2)}, u32[]{:S(2)}) async-start(bf16[32,2,16,256]{3,2,1,0:T(8,128)(2,1)} %copy.79), calls=%async_computation | async-start | bytes 1048576 | tf_op jit(solution)/shard_map/all_to_all | solution.py:118
  210.6 0.1 fusion.56
  210.7 0.1 copy.84
  210.8 0.1 fusion.54
  210.9 0.1 copy.85
  211.0 73.7 %all_gather.23 = f32[32,2,16,16]{3,2,1,0:T(8,128)S(1)} all-gather(f32[1,2,16,16]{3,2,1,0:T(8,128)S(1)} %pad_maximum_fusion), channel_id=1, replica_groups=mesh['band'=8,'col'=4] {'col','band'}, dimensions={0}, use_global_device_ids=true | all-gather | bytes 67584 | tf_op jit(solution)/shard_map/all_gather | solution.py:112
  284.7 0.1 copy.103
  284.9 0.1 copy.87
  285.0 0.1 neg.47
  285.1 0.1 slice.44
  285.2 0.1 reshape.279
  285.4 0.0 all-to-all-done
  285.4 0.1 reduce_sum.30
  285.5 0.9 convolution_bitcast_fusion
  (23 shorter events, 0.3 us)
Async XLA Ops:
  6.5 70.3 %all-gather.4.cloned.1.call-start = ((), (), s32[]{:S(2)}) async-start(), calls=%async_computation.1 | async-start | bytes 3981312 | tf_op jit(solution)/shard_map/all_gather | solution.py:68
  179.6 11.9 %copy-start = (bf16[2,4,2048,384]{3,2,1,0:T(8,128)(2,1)S(1)}, bf16[2,4,2048,384]{3,2,1,0:T(8,128)(2,1)}, u32[]{:S(2)}) copy-start(bf16[2,4,2048,384]{3,2,1,0:T(8,128)(2,1)} %convert_bitcast_fusion) | copy-start | bytes 37748740
  207.3 78.1 %all-to-all-start = ((bf16[32,2,16,256]{3,2,1,0:T(8,128)(2,1)}), bf16[32,2,16,256]{3,2,1,0:T(8,128)(2,1)S(1)}, u32[]{:S(2)}, u32[]{:S(2)}) async-start(bf16[32,2,16,256]{3,2,1,0:T(8,128)(2,1)} %copy.79), calls=%async_computation | async-start | bytes 1048576 | tf_op jit(solution)/shard_map/all_to_all | solution.py:118
Sparse Core Ops, SparseCore 0:
  9.5 67.3 all-gather.3
where the time goes:
time: 294 us; the launch traced here: 293 us
  matrix products  96 us (33%)
  blocking collectives  85.4 us (29%)
  waiting for transfers between devices  43.3 us (15%)
  local copies, waits for them, and re-layouts  32.5 us (11%)
  other arithmetic  18.3 us (6%)
  between operations  14.3 us (5%)
  starting transfers between devices  3.33 us (1%)
    all_gather x1, blocking collectives, per_device(): lax.all_gather(block_part, both, axis=0)  73.7 us
    all_gather x1, waiting for transfers between devices, per_device(): conduction_all = lax.all_gather(conduction_wave, 'band', axis=0, tiled=True)  42.6 us
    dot_general x2, matrix products, partial_density(): jnp.einsum('ogc,socn->sogn', one_hot(cells % slab, slab), planes, preferr...  42.4 us
    dot_general x1, matrix products, per_device(): jnp.einsum('srjy,rkyn->sjkn', y_table, z_done, preferred_element_type=f32)  19 us
    dot_general x4, matrix products, partial_density(): jnp.einsum('ogn,np->pog', part, fold, preferred_element_type=f32)  17 us
    convert_element_type x1, local copies, waits for them, and re-layouts, per_device(): jnp.einsum('srjy,rkyn->sjkn', y_table, z_done, preferred_element_type=f32)  15.2 us
    transpose x1, local copies, waits for them, and re-layouts, per_device(): products.reshape(lanes, plane_size).T.reshape(grid_y, grid_z, lanes)  10.3 us
    dot_general x1, matrix products, per_device(): jnp.einsum('rkz,yzn->rkyn', z_table, products, preferred_element_type=f32)  10 us
  transfers between devices with their start and end apart: 2, of which 1 were waited for; matrix products, arithmetic and copies ran while one was open for 5% of the time, Pallas kernels for 0%

commit v1 on v0

v1 whole, which is shorter than its diff:
```python
import functools
import math

import jax
import jax.numpy as jnp
import numpy as np
from jax import lax
from jax.experimental import pallas as pl
from jax.experimental.pallas import tpu as pltpu
from jax.sharding import PartitionSpec as P

GY = 96
LANE = 128
SUB = 8
INNER = 2
STEPS = 4
MESH = pl.DeviceIdType.MESH
VMEM_LIMIT = 62 * 1024 * 1024


def up(n, k):
    return -(-n // k) * k


def rounded(a):
    return jnp.asarray(a, jnp.bfloat16)


def angles(rows, cols, length):
    return 2.0 * math.pi * ((np.outer(rows, cols) % length) / length)


class Plan:
    def __init__(self, v_own, c_own, slab_x, plane, cols, bands, rows_all, blocks_all):
        self.inner = INNER if bands % INNER == 0 else 1
        self.outer = bands // self.inner
        self.v_own, self.c_own = v_own, c_own
        self.nv, self.nc, self.slab_x = v_own * self.inner, c_own * self.outer, slab_x
        self.gy, self.gz, self.gx = GY, plane // GY, slab_x * cols
        self.cols, self.bands = cols, bands
        self.pairs = self.nv * self.nc
        self.lanes = self.pairs * slab_x
        self.lanes_pad = up(self.lanes, LANE)
        self.chunks = self.lanes_pad // LANE
        self.tile = up(2 * self.chunks, SUB)
        self.half = self.gz // 2 + 1
        self.zrows = up(2 * self.half, SUB)
        self.group_lanes = self.gz * LANE // math.gcd(self.gz, LANE)
        self.group = self.group_lanes // self.gz
        self.dests = cols * bands
        self.rows_dest = rows_all // self.dests
        self.pack = LANE // (2 * self.pairs)
        self.rows_packed = self.rows_dest // self.pack
        self.blocks = blocks_all
        self.steps = STEPS
        self.block_packed = up(blocks_all, self.pack) // self.pack
        self.block_rows = up(self.block_packed, 2 * SUB)
        self.code_split = up(self.gx + 1, LANE)

    def windows(self):
        out, y = [], 0
        while y < self.group:
            start = y * self.gz // LANE * LANE
            ys = []
            while y < self.group and (y + 1) * self.gz <= start + 2 * LANE:
                ys.append(y)
                y += 1
            width = up(ys[-1] * self.gz + self.gz - start, LANE)
            out.append((start, width, ys))
        return out

    def z_tables(self):
        ang = angles(np.arange(self.half), np.arange(self.gz), self.gz)
        one = np.zeros((self.zrows, self.gz), np.float32)
        one[: self.half] = np.cos(ang)
        one[self.half : 2 * self.half] = -np.sin(ang)
        tables = []
        for start, width, ys in self.windows():
            t = np.zeros((len(ys) * self.zrows, width), np.float32)
            for i, y in enumerate(ys):
                lo = y * self.gz - start
                t[i * self.zrows : (i + 1) * self.zrows, lo : lo + self.gz] = one
            tables.append(rounded(t))
        return tables

    def y_table(self):
        ang = angles(np.arange(self.gy), np.arange(self.gy), self.gy)
        scale = 1.0 / math.sqrt(self.gy * self.gz)
        cos, sin = np.cos(ang) * scale, -np.sin(ang) * scale
        return rounded(np.block([[cos, -sin], [sin, cos]]))

    def x_tables(self):
        wide = 2 * self.lanes_pad
        out = np.zeros((self.cols, self.code_split, wide + LANE), np.float32)
        out[:, : self.gx, wide:] = 1.0
        out[:, self.gx, wide + self.pairs :] = -2.0
        scale = 1.0 / math.sqrt(self.gx)
        for col in range(self.cols):
            xs = col * self.slab_x + np.arange(self.lanes) % self.slab_x
            ang = angles(np.arange(self.gx), xs, self.gx)
            out[col, : self.gx, : self.lanes] = np.cos(ang) * scale
            out[col, : self.gx, self.lanes_pad : self.lanes_pad + self.lanes] = -np.sin(ang) * scale
        return rounded(out)

    def fold_table(self):
        out = np.zeros((2 * self.lanes_pad, LANE), np.float32)
        n = np.arange(self.lanes)
        out[n, n // self.slab_x] = 1.0
        out[self.lanes_pad + n, self.pairs + n // self.slab_x] = 1.0
        return rounded(out)


def density_kernel(p, pidx, v_own, v_far, c_own, c_far, code_ref, *refs):
    n_win = len(p.windows())
    zt_refs = refs[:n_win]
    yt_ref, xt_ref, fold_ref, out_ref, z_ref, planes_ref, pick_ref, v_ref, c_ref, sem = refs[n_win:]
    f32, bf16 = jnp.float32, jnp.bfloat16
    sx = p.slab_x

    outer, inner = place(p)
    copies = []
    for own, far, dst, n, me in ((v_own, v_far, v_ref, p.inner, inner), (c_own, c_far, c_ref, p.outer, outer)):
        size = own.shape[0]
        for d in range(n):
            src = own if d == 0 else far.at[d - 1]
            slot = lax.rem(me + d, n) * size
            copies.append(pltpu.make_async_copy(src, dst.at[pl.ds(slot, size)], sem.at[len(copies)]))
    for copy in copies:
        copy.start()
    for copy in copies:
        copy.wait()

    def z_step(q, carry):
        lanes = pl.ds(pl.multiple_of(q * p.group_lanes, LANE), p.group_lanes)
        v = v_ref[:, :, lanes].astype(f32)
        c = c_ref[:, :, lanes].astype(f32)
        parts = [v[i] * c[j] for i in range(p.nv) for j in range(p.nc)]
        if p.lanes_pad > p.lanes:
            parts.append(jnp.zeros((p.lanes_pad - p.lanes, p.group_lanes), f32))
        prod = jnp.concatenate(parts, axis=0).astype(bf16)
        for t_ref, (start, width, ys) in zip(zt_refs, p.windows()):
            z = lax.dot_general(
                t_ref[...],
                prod[:, start : start + width],
                (((1,), (1,)), ((), ())),
                preferred_element_type=f32,
            )
            rows = len(ys) * p.zrows
            base = pl.multiple_of((q * p.group + ys[0]) * p.zrows, SUB)
            for j in range(p.chunks):
                z_ref[j, pl.ds(base, rows), :] = z[:, j * LANE : (j + 1) * LANE]
        return carry

    lax.fori_loop(0, p.gy // p.group, z_step, 0)

    def y_step(kz, carry):
        cols = []
        for j in range(p.chunks):
            parts = [
                z_ref[j, pl.ds(r * p.half + kz, p.gy, stride=p.zrows), :] for r in range(2)
            ]
            cols.append(jnp.concatenate(parts, axis=0).astype(bf16))
        rhs = jnp.concatenate(cols, axis=1)
        out = jnp.dot(yt_ref[...], rhs, preferred_element_type=f32)
        for s in range(2):
            for j in range(p.chunks):
                planes_ref[pl.ds(kz * (p.gy * p.tile) + s * p.chunks + j, p.gy, stride=p.tile), :] = out[
                    s * p.gy : (s + 1) * p.gy, j * LANE : (j + 1) * LANE
                ]
        return carry

    lax.fori_loop(0, p.half, y_step, 0)

    col = lax.axis_index("col")

    def density(d, rows):
        def pick(i, carry):
            for u in range(16):
                g = i * 16 + u
                src = pl.multiple_of(pidx[d * p.rows_dest + g], SUB)
                pick_ref[pl.ds(pl.multiple_of(g * p.tile, SUB), p.tile), :] = planes_ref[pl.ds(src, p.tile), :]
            return carry

        lax.fori_loop(0, rows // 16, pick, 0)
        code = code_ref[pl.ds(d, 1), :rows]
        mirror = code >= p.code_split
        kx = jnp.where(mirror, code - p.code_split, code)
        span = lax.broadcasted_iota(jnp.int32, (p.code_split, rows), 0)
        hot = jnp.where((span == kx) | ((span == p.gx) & mirror), 1.0, 0.0).astype(bf16)
        phase = lax.dot_general(
            hot, xt_ref[col], (((0,), (0,)), ((), ())), preferred_element_type=f32
        )
        real, imag = [], []
        for j in range(p.chunks):
            re = pick_ref[pl.ds(j, rows, stride=p.tile), :]
            im = pick_ref[pl.ds(p.chunks + j, rows, stride=p.tile), :]
            cos = phase[:, j * LANE : (j + 1) * LANE]
            sin = phase[:, p.lanes_pad + j * LANE : p.lanes_pad + (j + 1) * LANE]
            real.append((cos * re - sin * im).astype(bf16))
            imag.append((sin * re + cos * im).astype(bf16))
        turned = jnp.concatenate(real + imag, axis=1)
        folded = jnp.dot(turned, fold_ref[...], preferred_element_type=f32)
        return folded * phase[:, 2 * p.lanes_pad :]

    def packed(full, rows):
        step = rows // p.pack
        total = full[:step]
        for q in range(1, p.pack):
            total = total + pltpu.roll(full[q * step : (q + 1) * step], q * 2 * p.pairs, 1)
        return total

    def row_step(d, carry):
        out_ref[d] = packed(density(d, p.rows_dest), p.rows_dest).astype(bf16)
        return carry

    lax.fori_loop(0, p.dests + 1, row_step, 0)


def density_call(p, pidx, code, v_own, v_far, c_own, c_far):
    tables = p.z_tables() + [p.y_table(), p.x_tables(), p.fold_table()]
    vmem = pl.BlockSpec(memory_space=pltpu.VMEM)
    return pl.pallas_call(
        functools.partial(density_kernel, p),
        out_shape=jax.ShapeDtypeStruct((p.dests + 1, p.rows_packed, LANE), jnp.bfloat16),
        in_specs=[pl.BlockSpec(memory_space=pltpu.SMEM)]
        + [pl.BlockSpec(memory_space=pl.ANY)] * 4
        + [vmem] * (1 + len(tables)),
        out_specs=vmem,
        scratch_shapes=[
            pltpu.VMEM((p.chunks, p.gy * p.zrows, LANE), jnp.float32),
            pltpu.VMEM((p.half * p.gy * p.tile, LANE), jnp.float32),
            pltpu.VMEM((p.rows_dest * p.tile, LANE), jnp.float32),
            pltpu.VMEM((p.nv, p.slab_x, p.gy * p.gz), jnp.bfloat16),
            pltpu.VMEM((p.nc, p.slab_x, p.gy * p.gz), jnp.bfloat16),
            pltpu.SemaphoreType.DMA((p.inner + p.outer,)),
        ],
        compiler_params=pltpu.CompilerParams(vmem_limit_bytes=VMEM_LIMIT),
        name="density",
    )(pidx, v_own, v_far, c_own, c_far, code, *tables)


def lookups(p, cells, blocks):
    slab_y = p.gy // p.cols

    def points(values):
        owner = lax.broadcasted_iota(jnp.int32, values.shape, 0)
        kx = values // (slab_y * p.gz)
        ky = owner * slab_y + values // p.gz % slab_y
        kz = values % p.gz
        mirror = kz >= p.half
        kx = jnp.where(mirror & (kx > 0), p.gx - kx, kx)
        ky = jnp.where(mirror & (ky > 0), p.gy - ky, ky)
        kz = jnp.where(mirror, p.gz - kz, kz)
        return (kz * p.gy + ky) * p.tile, kx + jnp.where(mirror, p.code_split, 0)

    pencil, code = points(cells)
    m = np.arange(p.blocks)
    slot = m // p.block_packed * p.rows_packed + m % p.block_packed
    spread = np.zeros((p.rows_dest,), np.int32)
    spread[slot] = m
    hot = jnp.asarray(spread[None, :] == m[:, None])

    def last(a):
        return jnp.sum(jnp.where(hot, a.reshape(-1, 1), 0), axis=0)[None]

    block_pencil, block_code = points(blocks)
    pencil = jnp.concatenate([pencil.reshape(-1, p.rows_dest), last(block_pencil)], axis=0)
    code = jnp.concatenate([code.reshape(-1, p.rows_dest), last(block_code)], axis=0)
    return pencil.reshape(-1), code


def place(p):
    band = lax.axis_index("band")
    return band // p.inner, lax.rem(band, p.inner)


def meet(targets):
    barrier = pltpu.get_barrier_semaphore()
    for target in targets:
        pl.semaphore_signal(barrier, inc=1, device_id=target, device_id_type=MESH)
    pl.semaphore_wait(barrier, len(targets))


def gather_kernel(p, v_in, c_in, cell_in, block_in, v_out, c_out, cell_out, block_out, vs, vr, cs, cr, cell_sem):
    outer, inner = place(p)
    col = lax.axis_index("col")
    at = lambda o, i: (o * p.inner + i, col)
    lanes = v_in.shape[2] // p.steps

    def cut(ref, step):
        return ref.at[:, :, pl.ds(step * lanes, lanes)]

    inner_ids = [at(outer, lax.rem(inner + d, p.inner)) for d in range(1, p.inner)]
    up_id, down_id = (at(lax.rem(outer + s, p.outer), inner) for s in (1, p.outer - 1))
    col_ids = [(lax.axis_index("band"), lax.rem(col + d, p.cols)) for d in range(1, p.cols)]
    meet(inner_ids + [up_id, down_id] + col_ids)

    cell_copies = []
    for d, target in enumerate(col_ids):
        for k, (src, dst) in enumerate(((cell_in, cell_out), (block_in, block_out))):
            cell_copies.append(
                pltpu.make_async_remote_copy(
                    src, dst.at[col], cell_sem.at[0, d, k], cell_sem.at[1, d, k], device_id=target, device_id_type=MESH
                )
            )
    mine = [
        pltpu.make_async_copy(src, dst.at[col], cell_sem.at[0, p.cols - 1, k])
        for k, (src, dst) in enumerate(((cell_in, cell_out), (block_in, block_out)))
    ]
    v_copies = [
        [
            pltpu.make_async_remote_copy(
                cut(v_in, step),
                cut(v_out.at[p.inner - d - 1], step),
                vs.at[d - 1, step],
                vr.at[p.inner - d - 1, step],
                device_id=target,
                device_id_type=MESH,
            )
            for step in range(p.steps)
        ]
        for d, target in enumerate(inner_ids, 1)
    ]

    def hop(way, d, step):
        if way == 0:
            slot, target = p.outer - 1 - d - 1, up_id
            src = c_in if d == 0 else c_out.at[p.outer - d - 1]
        else:
            slot, target = d, down_id
            src = c_in if d == 0 else c_out.at[d - 1]
        return pltpu.make_async_remote_copy(
            cut(src, step),
            cut(c_out.at[slot], step),
            cs.at[way, d, step],
            cr.at[slot, step],
            device_id=target,
            device_id_type=MESH,
        )

    def sends(way, d):
        if way == 0:
            return (outer >= d) & (outer < p.outer - 1)
        return (outer + d < p.outer) & (outer > 0)

    def arrival(way, d, step):
        return hop(way, d - 1, step)

    for step in range(p.steps):
        for way in range(2):

            @pl.when(sends(way, 0))
            def _():
                hop(way, 0, step).start()

        for copies in v_copies:
            copies[step].start()
        if step == 0:
            for copy in cell_copies + mine:
                copy.start()
    for d in range(1, p.outer - 1):
        for step in range(p.steps):
            for way in range(2):

                @pl.when(sends(way, d))
                def _():
                    arrival(way, d, step).wait_recv()
                    hop(way, d, step).start()

    for way in range(2):
        for d in range(1, p.outer):
            last = (outer == p.outer - 1) if way == 0 else (outer == 0)

            @pl.when(last)
            def _():
                for step in range(p.steps):
                    arrival(way, d, step).wait_recv()

    for way in range(2):
        for d in range(p.outer - 1):

            @pl.when(sends(way, d))
            def _():
                for step in range(p.steps):
                    hop(way, d, step).wait_send()

    for copies in v_copies:
        for copy in copies:
            copy.wait()
    for copy in cell_copies + mine:
        copy.wait()


def gather_call(p, v, c, cells, blocks):
    hbm = pl.BlockSpec(memory_space=pl.ANY)
    dma = pltpu.SemaphoreType.DMA
    out = [
        jax.ShapeDtypeStruct((p.inner - 1,) + v.shape, v.dtype),
        jax.ShapeDtypeStruct((p.outer - 1,) + c.shape, c.dtype),
        jax.ShapeDtypeStruct((p.cols,) + cells.shape, cells.dtype),
        jax.ShapeDtypeStruct((p.cols,) + blocks.shape, blocks.dtype),
    ]
    return pl.pallas_call(
        functools.partial(gather_kernel, p),
        out_shape=out,
        in_specs=[hbm] * 4,
        out_specs=[hbm] * 4,
        scratch_shapes=[
            dma((p.inner - 1, p.steps)),
            dma((p.inner - 1, p.steps)),
            dma((2, p.outer - 1, p.steps)),
            dma((p.outer - 1, p.steps)),
            dma((2, p.cols, 2)),
        ],
        compiler_params=pltpu.CompilerParams(collective_id=0, has_side_effects=True),
        name="gather",
    )(v, c, cells, blocks)


def exchange_kernel(p, part_ref, row_out, block_out, send_sem, recv_sem):
    col, band = lax.axis_index("col"), lax.axis_index("band")
    me = col * p.bands + band

    def target(d):
        other = lax.rem(me + d, p.dests)
        return other, (lax.rem(other, p.bands), other // p.bands)

    barrier = pltpu.get_barrier_semaphore()

    def greet(d, carry):
        pl.semaphore_signal(barrier, inc=1, device_id=target(d)[1], device_id_type=MESH)
        return carry

    lax.fori_loop(1, p.dests, greet, 0)
    pl.semaphore_wait(barrier, p.dests - 1)

    def copies(d):
        other, where = target(d)
        tail = part_ref.at[p.dests, pl.ds(0, p.block_rows)]
        return [
            pltpu.make_async_remote_copy(
                src, dst, send_sem.at[d, k], recv_sem.at[d, k], device_id=where, device_id_type=MESH
            )
            for k, (src, dst) in enumerate(((part_ref.at[other], row_out.at[me]), (tail, block_out.at[me])))
        ]

    def start(d, carry):
        for copy in copies(d):
            copy.start()
        return carry

    lax.fori_loop(1, p.dests, start, 0)
    row_out[pl.ds(me, 1)] = part_ref[pl.ds(me, 1)]
    block_out[pl.ds(me, 1)] = part_ref[p.dests :, : p.block_rows]

    def finish(d, carry):
        for copy in copies(d):
            copy.wait()
        return carry

    lax.fori_loop(1, p.dests, finish, 0)


def exchange_call(p, part):
    vmem = pl.BlockSpec(memory_space=pltpu.VMEM)
    dma = pltpu.SemaphoreType.DMA
    return pl.pallas_call(
        functools.partial(exchange_kernel, p),
        out_shape=[
            jax.ShapeDtypeStruct((p.dests, p.rows_packed, LANE), part.dtype),
            jax.ShapeDtypeStruct((p.dests, p.block_rows, LANE), part.dtype),
        ],
        in_specs=[vmem],
        out_specs=[vmem, vmem],
        scratch_shapes=[dma((p.dests, 2)), dma((p.dests, 2))],
        compiler_params=pltpu.CompilerParams(collective_id=1, has_side_effects=True),
        name="exchange",
    )(part)


def polarizability(p, rows_in, blocks_in, weights):
    f32, bf16 = jnp.float32, jnp.bfloat16

    def total(parts):
        parts = parts.reshape((p.cols, p.bands) + parts.shape[1:]).astype(f32)
        return jnp.sum(parts, axis=0).astype(bf16)

    rows = total(rows_in)
    block = total(blocks_in)[:, : p.block_packed].astype(f32)
    block = block.reshape(p.bands, p.block_packed, p.pack, 2, p.pairs)
    block = block.transpose(0, 3, 4, 2, 1).reshape(p.bands, 2, p.pairs, p.pack * p.block_packed)[..., : p.blocks]
    real, imag = block[:, 0], block[:, 1]
    pair = jnp.stack([jnp.stack([real, -imag], axis=2), jnp.stack([imag, real], axis=2)], axis=1)
    right = pair[:, :, :, None] * weights.transpose(0, 2, 1)[:, None, :, :, None, None]
    right = right.astype(bf16).reshape(p.bands, 1, 2 * p.pairs, 1, -1)
    eye = jnp.asarray(np.eye(p.pack).reshape(1, p.pack, 1, p.pack, 1), bf16)
    right = (eye * right).reshape(p.bands * LANE, -1)
    left = rows.transpose(1, 0, 2).reshape(p.rows_packed, p.bands * LANE)
    chi = jnp.dot(left, right, preferred_element_type=f32)
    return chi.reshape(p.rows_packed, p.pack, -1).transpose(1, 0, 2).reshape(p.rows_dest, -1)


def pair_weights(p, valence_index, occupied_energy, conduction_energy, frequency):
    span = jnp.arange(occupied_energy.shape[0], dtype=jnp.int32)
    hit = valence_index[:, None] == span[None, :]
    valence_energy = jnp.sum(jnp.where(hit, occupied_energy[None, :], 0.0), axis=1)
    gap = conduction_energy[None, :] - valence_energy[:, None]
    freq = frequency[:, None, None]
    norm = 1.0 / math.sqrt(gap.size)
    weights = -4.0 * gap[None] / (gap[None] * gap[None] + freq * freq) * norm
    split = weights.reshape(-1, p.outer, p.nv, p.outer, p.inner, p.c_own)
    return split.transpose(1, 4, 0, 2, 3, 5).reshape(p.bands, -1, p.pairs)


def per_device(
    valence_wave,
    conduction_wave,
    valence_index,
    occupied_energy,
    conduction_energy,
    frequency,
    gvec_cell,
    block_cell,
):
    cols, bands = lax.axis_size("col"), lax.axis_size("band")
    p = Plan(
        valence_wave.shape[0],
        conduction_wave.shape[0],
        valence_wave.shape[1],
        valence_wave.shape[2],
        cols,
        bands,
        gvec_cell.shape[0] * cols,
        block_cell.shape[0] * cols,
    )
    weights = pair_weights(p, valence_index, occupied_energy, conduction_energy, frequency)
    v_far, c_far, cells, blocks = gather_call(
        p, valence_wave, conduction_wave, gvec_cell.reshape(-1, LANE), block_cell.reshape(1, -1)
    )
    pencil, code = lookups(p, cells.reshape(cols, -1), blocks.reshape(cols, -1))
    part = density_call(p, pencil, code, valence_wave, v_far, conduction_wave, c_far)
    rows, block = exchange_call(p, part)
    return polarizability(p, rows, block, weights)


def solution(mesh):
    return jax.shard_map(
        per_device,
        mesh=mesh,
        in_specs=(
            P("band", "col", None),
            P("band", "col", None),
            P(),
            P(),
            P(),
            P(),
            P("col"),
            P("col"),
        ),
        out_specs=P(("col", "band"), None),
        check_vma=False,
    )
```

time: 294 us -> 126 us (0.43)
  Pallas kernels: 0 us -> 114 us
  matrix products: 96 us -> 1.1 us
  blocking collectives: 85.4 us -> 0 us
  waiting for transfers between devices: 43.3 us -> 0 us
  local copies, waits for them, and re-layouts: 32.5 us -> 3.83 us
  between operations: 14.3 us -> 0.29 us
  other arithmetic: 18.3 us -> 6.5 us
  starting transfers between devices: 3.33 us -> 0 us
    pallas_call x0 -> x3, Pallas kernels: none -> 114 us  [the longest x1 57 us: density_call(): pl.pallas_call(functools.partial(density_kernel, p), out_shape=jax.ShapeD...]
    dot_general x11 -> x1, matrix products: 96 us -> 1.1 us  [polarizability(): chi = jnp.dot(left, right, preferred_element_type=f32)]
    all_gather x2 -> x0, blocking collectives: 79.1 us -> none  [the longest x1 73.7 us: per_device(): lax.all_gather(block_part, both, axis=0)]
    all_gather x1 -> x0, waiting for transfers between devices: 42.6 us -> none  [per_device(): conduction_all = lax.all_gather(conduction_wave, 'band', axis=0, tiled=True)]
    convert_element_type x3 -> x1, local copies, waits for them, and re-layouts: 15.3 us -> 0.34 us  [polarizability(): right = right.astype(bf16).reshape(p.bands, 1, 2 * p.pairs, 1, -1)]
    convert_element_type x8 -> x1, other arithmetic: 15.2 us -> 0.72 us  [polarizability(): right = right.astype(bf16).reshape(p.bands, 1, 2 * p.pairs, 1, -1)]
    transpose x3 -> x1, local copies, waits for them, and re-layouts: 11.4 us -> 0.09 us  [polarizability(): left = rows.transpose(1, 0, 2).reshape(p.rows_packed, p.bands * LANE)]
    unnamed x1 -> x0, blocking collectives: 6.38 us -> none
  transfers between devices with their start and end apart: 2 -> 0, of which waited for: 1 -> 0; matrix products, arithmetic and copies ran while one was open for 5% -> 0% of each run, Pallas kernels for 0% -> 0%
where the time goes in v1:
time: 126 us; the launch traced here: 125 us
  Pallas kernels  114 us (90%)
  other arithmetic  6.5 us (5%)
  local copies, waits for them, and re-layouts  3.83 us (3%)
    pallas_call x1, Pallas kernels, density_call(): pl.pallas_call(functools.partial(density_kernel, p), out_shape=jax.ShapeD...  57 us
    pallas_call x1, Pallas kernels, gather_call(): pl.pallas_call(functools.partial(gather_kernel, p), out_shape=out, in_spe...  34.9 us
    pallas_call x1, Pallas kernels, exchange_call(): pl.pallas_call(functools.partial(exchange_kernel, p), out_shape=[jax.Shap...  21.7 us

profile of v1, /device:TPU:0, one launch (start us, length us, event | category | flops | bytes accessed | tf_op | source)
XLA Modules:
  0.0 125.3 jit_solution(6996205466127563284)
XLA Ops:
  0.0 0.0 copy-start.2
  0.0 34.9 %gather.1 = (bf16[1,2,24,9216]{3,2,1,0:T(8,128)(2,1)}, bf16[3,1,24,9216]{3,2,1,0:T(8,128)(2,1)}, s32[4,16,128]{2,1,0:T(8,128)}, s32[4,1,4]{2,1,0:T(1,128)}) custom-call(bf16[2,24,9216]{2,1,0:T(8,128)(2,1)} %v_own.1, bf16[1,24,9216]{2,1,0:T(8,128)(2,1)} %c_own.1, s32[16,128]{1,0:T(8,128)} %bitcast.50, s32[1,4]{1,0:T(1,128)} %bitcast.53), custom_call_target="tpu_custom_call" | custom-call | tf_op jit(solution)/shard_map/gather/pallas_call | solution.py:403
  34.9 0.7 divide_reduce_fusion
  35.6 0.1 div.60
  35.7 0.1 div.64
  35.8 0.1 rem.89
  35.8 0.7 compare_reduce_fusion
  36.5 0.1 ne.123
  36.6 0.1 ne.128
  36.7 0.1 iota.26
  36.8 0.1 iota.27
  36.9 0.0 copy-done.2
  36.9 0.1 select_reduce_fusion.1
  37.0 0.8 broadcast_divide_fusion
  37.8 0.8 remainder_compare_fusion
  38.7 0.1 iota.23
  38.7 0.1 iota.24
  38.8 0.1 fusion.5
  38.9 0.6 pad_add_fusion
  39.6 0.6 reshape.249.pidx
  40.2 57.0 %density.1.part_ref = bf16[33,64,128]{2,1,0:T(8,128)(2,1)} custom-call(s32[8448]{0:T(1024)} %reshape.249.pidx, bf16[2,24,9216]{2,1,0:T(8,128)(2,1)} %v_own.1, bf16[1,2,24,9216]{3,2,1,0:T(8,128)(2,1)} %get-tuple-element.13.v_far, bf16[1,24,9216]{2,1,0:T(8,128)(2,1)} %c_own.1, bf16[3,1,24,9216]{3,2,1,0:T(8,128)(2,1)} %get-tuple-element.14.c_far, ...), custom_call_target="tpu_custom_call" | custom-call | tf_op jit(solution)/shard_map/density/pallas_call | solution.py:222
  97.1 21.7 %exchange.1 = (bf16[32,64,128]{2,1,0:T(8,128)(2,1)}, bf16[32,16,128]{2,1,0:T(8,128)(2,1)}) custom-call(bf16[33,64,128]{2,1,0:T(8,128)(2,1)} %density.1.part_ref), custom_call_target="tpu_custom_call" | custom-call | tf_op jit(solution)/shard_map/exchange/pallas_call | solution.py:467
  118.9 0.0 copy-start.4
  118.9 0.0 copy-start.1
  118.9 0.0 copy-start.5
  118.9 0.0 copy-start.6
  118.9 0.9 reduce_sum.54
  119.9 0.2 reshape.262
  120.2 0.0 copy-start.3
  120.3 0.2 copy.45
  120.4 0.0 copy-done.4
  120.5 0.1 sub.84
  120.5 0.1 copy.46
  120.6 0.0 copy-done.1
  120.6 0.0 copy-done.5
  120.6 0.2 select_reduce_fusion
  120.9 0.1 sub.86
  121.0 0.1 subtract_multiply_fusion.1
  121.0 0.0 copy-done.6
  121.0 0.1 divide_multiply_fusion
  121.2 0.7 multiply_convert_fusion
  121.9 0.3 convert_element_type.16
  122.2 0.0 copy-done.3
  122.3 0.5 broadcast_multiply_fusion
  122.7 0.2 copy.53
  122.9 0.0 copy-start
  122.9 0.5 copy.48
  123.5 0.5 copy-done
  124.0 0.1 reduce_sum.53
  124.0 0.1 copy.42
  124.1 0.1 reshape.263
  124.2 1.1 fusion.11
  (15 shorter events, 0.2 us)
Async XLA Ops:
  0.0 36.9 %copy-start.2 = (pred[16,256]{1,0:T(8,128)(4,1)S(1)}, pred[16,256]{1,0:T(8,128)(4,1)}, u32[]{:S(2)}) copy-start(pred[16,256]{1,0:T(8,128)(4,1)} %constant.89.clone) | copy-start | bytes 12292
  118.9 1.6 %copy-start.4 = (f32[8]{0:T(128)S(1)}, f32[8]{0:T(128)}, u32[]{:S(2)}) copy-start(f32[8]{0:T(128)} %param.19) | copy-start | bytes 100
  118.9 1.7 %copy-start.1 = (f32[4096]{0:T(1024)S(1)}, f32[4096]{0:T(1024)}, u32[]{:S(2)}) copy-start(f32[4096]{0:T(1024)} %param.18) | copy-start | bytes 49156
  118.9 1.7 %copy-start.5 = (s32[16]{0:T(128)S(1)}, s32[16]{0:T(128)}, u32[]{:S(2)}) copy-start(s32[16]{0:T(128)} %param.17) | copy-start | bytes 196
  118.9 2.1 %copy-start.6 = (f32[4]{0:T(128)S(1)}, f32[4]{0:T(128)}, u32[]{:S(2)}) copy-start(f32[4]{0:T(128)} %param.20) | copy-start | bytes 52
  120.2 2.0 %copy-start.3 = (bf16[4,4]{1,0:T(4,128)(2,1)S(1)}, bf16[4,4]{1,0:T(4,128)(2,1)}, u32[]{:S(2)}) copy-start(bf16[4,4]{1,0:T(4,128)(2,1)} %constant.98) | copy-start | bytes 100
  122.9 1.0 copy-start

commit v2 on v0

v2 whole, which is shorter than its diff:
```python
import functools
import math

import jax
import jax.numpy as jnp
import numpy as np
from jax import lax
from jax.experimental import pallas as pl
from jax.experimental.pallas import tpu as pltpu
from jax.sharding import PartitionSpec as P

GY = 96
LANE = 128
SUB = 8
INNER = 2
STEPS = 6
MESH = pl.DeviceIdType.MESH
VMEM_LIMIT = 66_000_000


def up(n, k):
    return -(-n // k) * k


def rounded(a):
    return jnp.asarray(a, jnp.bfloat16)


def angles(rows, cols, length):
    return 2.0 * math.pi * ((np.outer(rows, cols) % length) / length)


class Plan:
    def __init__(self, v_own, c_own, slab_x, plane, cols, bands, rows_all, blocks_all, freqs):
        self.inner = INNER if bands % INNER == 0 else 1
        self.outer = bands // self.inner
        self.v_own, self.c_own = v_own, c_own
        self.nv, self.nc, self.slab_x = v_own * self.inner, c_own * self.outer, slab_x
        self.gy, self.gz, self.gx = GY, plane // GY, slab_x * cols
        self.cols, self.bands, self.freqs = cols, bands, freqs
        self.pairs = self.nv * self.nc
        self.lanes = self.pairs * slab_x
        self.lanes_pad = up(self.lanes, LANE)
        self.chunks = self.lanes_pad // LANE
        self.tile = up(2 * self.chunks, SUB)
        self.pitch = self.tile + 1
        self.half = self.gz // 2 + 1
        self.zrows = up(2 * self.half, SUB)
        self.zpitch = self.zrows + 1
        self.group_lanes = self.gz * LANE // math.gcd(self.gz, LANE)
        self.group = self.group_lanes // self.gz
        self.dests = cols * bands
        self.rows_dest = rows_all // self.dests
        self.halves = self.rows_dest // LANE
        self.pack = LANE // (2 * self.pairs)
        self.rows_packed = self.rows_dest // self.pack
        self.cell_rows = rows_all // cols // LANE
        self.blocks = blocks_all
        self.block_rows = up(blocks_all, 2 * SUB)
        self.steps = STEPS
        self.code_rows = up(self.gx + 1, LANE)
        self.wide = 2 * self.lanes_pad + LANE

    def windows(self):
        out, y = [], 0
        while y < self.group:
            start = y * self.gz // LANE * LANE
            ys = []
            while y < self.group and (y + 1) * self.gz <= start + 2 * LANE:
                ys.append(y)
                y += 1
            width = up(ys[-1] * self.gz + self.gz - start, LANE)
            out.append((start, width, ys))
        return out

    def z_tables(self):
        ang = angles(np.arange(self.half), np.arange(self.gz), self.gz)
        one = np.zeros((self.zrows, self.gz), np.float32)
        one[: self.half] = np.cos(ang)
        one[self.half : 2 * self.half] = -np.sin(ang)
        tables = []
        for start, width, ys in self.windows():
            t = np.zeros((len(ys) * self.zrows, width), np.float32)
            for i, y in enumerate(ys):
                lo = y * self.gz - start
                t[i * self.zrows : (i + 1) * self.zrows, lo : lo + self.gz] = one
            tables.append(rounded(t))
        return tables

    def y_table(self):
        ang = angles(np.arange(self.gy), np.arange(self.gy), self.gy)
        scale = 1.0 / math.sqrt(self.gy * self.gz)
        cos, sin = np.cos(ang) * scale, -np.sin(ang) * scale
        return rounded(np.block([[cos, -sin], [sin, cos]]))

    def x_tables(self):
        wide = 2 * self.lanes_pad
        out = np.zeros((self.cols, self.code_rows, wide + LANE), np.float32)
        out[:, : self.gx, wide:] = 1.0
        out[:, self.gx, wide + self.pairs :] = -2.0
        scale = 1.0 / math.sqrt(self.gx)
        for col in range(self.cols):
            xs = col * self.slab_x + np.arange(self.lanes) % self.slab_x
            ang = angles(np.arange(self.gx), xs, self.gx)
            out[col, : self.gx, : self.lanes] = np.cos(ang) * scale
            out[col, : self.gx, self.lanes_pad : self.lanes_pad + self.lanes] = -np.sin(ang) * scale
        return rounded(out)

    def fold_table(self):
        out = np.zeros((2 * self.lanes_pad, LANE), np.float32)
        n = np.arange(self.lanes)
        out[n, n // self.slab_x] = 1.0
        out[self.lanes_pad + n, self.pairs + n // self.slab_x] = 1.0
        return rounded(out)


def place(p):
    band = lax.axis_index("band")
    return band // p.inner, lax.rem(band, p.inner)


def remote(src, dst, send, recv, target):
    return pltpu.make_async_remote_copy(src, dst, send, recv, device_id=target, device_id_type=MESH)


def kernel(p, v_in, c_in, cell_in, xt_in, weight_ref, *refs):
    n_win = len(p.windows())
    zt_refs = refs[:n_win]
    (yt_ref, fold_ref, chi_ref, z_ref, planes_ref, pick_a, pick_b, v_ref, c_ref, cells, pidx_v, pidx, code_ref,
     phase_ref, xt_ref, part_ref, row_ref, block_ref, own_sem, vs, vr, cs, cr, cell_sem, row_sem, block_sem) = refs[n_win:]
    f32, bf16, i32 = jnp.float32, jnp.bfloat16, jnp.int32
    outer, inner = place(p)
    col, band = lax.axis_index("col"), lax.axis_index("band")
    me = col * p.bands + band

    def device(d):
        return (lax.rem(d, p.bands), d // p.bands)

    barrier = pltpu.get_barrier_semaphore()

    def greet(k, carry):
        target = device(lax.rem(me + k, p.dests))
        pl.semaphore_signal(barrier, inc=1, device_id=target, device_id_type=MESH)
        return carry

    lax.fori_loop(1, p.dests, greet, 0)
    local = [
        pltpu.make_async_copy(v_in, v_ref.at[pl.ds(inner * p.v_own, p.v_own)], own_sem.at[0]),
        pltpu.make_async_copy(c_in, c_ref.at[pl.ds(outer * p.c_own, p.c_own)], own_sem.at[1]),
        pltpu.make_async_copy(cell_in, cells.at[col], own_sem.at[2]),
        pltpu.make_async_copy(xt_in.at[col], xt_ref, own_sem.at[3]),
    ]
    for copy in local:
        copy.start()
    pl.semaphore_wait(barrier, p.dests - 1)

    step_lanes = p.gy * p.gz // p.steps

    def cut(ref, step):
        return ref.at[:, :, pl.ds(step * step_lanes, step_lanes)]

    def v_copy(d, step):
        slot = v_ref.at[pl.ds(inner * p.v_own, p.v_own)]
        target = (outer * p.inner + lax.rem(inner + d, p.inner), col)
        return remote(cut(v_in, step), cut(slot, step), vs.at[d - 1, step], vr.at[d - 1, step], target)

    def hop(way, d, step):
        origin = lax.rem(outer + (p.outer - d if way == 0 else d), p.outer)
        slot = c_ref.at[pl.ds(origin * p.c_own, p.c_own)]
        target = (lax.rem(outer + (1 if way == 0 else p.outer - 1), p.outer) * p.inner + inner, col)
        src = c_in if d == 0 else slot
        return remote(cut(src, step), cut(slot, step), cs.at[way, d, step], cr.at[way, d, step], target)

    def arrives(way, d, step):
        origin = lax.rem(outer + (p.outer - d if way == 0 else d), p.outer)
        slot = c_ref.at[pl.ds(origin * p.c_own, p.c_own)]
        return remote(cut(slot, step), cut(slot, step), cs.at[way, d - 1, step], cr.at[way, d - 1, step], (band, col))

    reach = (p.outer - 1) // 2

    def ways(d, step):
        if d <= reach:
            return (0, 1)
        return (step % 2,) if 2 * d == p.outer else ()

    far = p.outer // 2
    cell_copies = []
    for d in range(1, p.cols):
        target = (band, lax.rem(col + d, p.cols))
        cell_copies.append(remote(cell_in, cells.at[col], cell_sem.at[0, d - 1], cell_sem.at[1, d - 1], target))
    for copy in cell_copies:
        copy.start()
    for step in range(p.steps):
        for way in ways(1, step):
            hop(way, 0, step).start()
        for d in range(1, p.inner):
            v_copy(d, step).start()

    for copy in local[2:]:
        copy.wait()
    for copy in cell_copies:
        copy.wait()
    slab_y = p.gy // p.cols

    def points(values, owner):
        def split(a, n):
            high = lax.div(a, jnp.full(a.shape, n, i32))
            return high, a - high * n

        kx, rest = split(values, slab_y * p.gz)
        ky, kz = split(rest, p.gz)
        ky = ky + owner * slab_y
        mirror = kz >= p.half
        kx = jnp.where(mirror & (kx > 0), p.gx - kx, kx)
        ky = jnp.where(mirror & (ky > 0), p.gy - ky, ky)
        kz = jnp.where(mirror, p.gz - kz, kz)
        return (kz * p.gy + ky) * p.pitch, kx + jnp.where(mirror, p.code_rows, 0)

    last = jnp.zeros((1, LANE), i32)
    lane_owner = jnp.zeros((1, LANE), i32)
    lane = lax.broadcasted_iota(i32, (1, LANE), 1)
    per_owner = p.blocks // p.cols
    for k in range(p.cols):
        rows = pl.ds(k * p.cell_rows, p.cell_rows)
        pencil, code = points(cells[k, : p.cell_rows, :], k)
        pidx_v[rows, :] = pencil
        code_ref[rows, :] = code
        row = cells[k, p.cell_rows : p.cell_rows + 1, :]
        last = last + (pltpu.roll(row, k * per_owner, 1) if k else row)
        lane_owner = lane_owner + jnp.where(lane >= k * per_owner, 1, 0)
    pencil, code = points(last, jnp.minimum(lane_owner - 1, p.cols - 1))
    for k in range(p.halves):
        at = p.dests * p.halves + k
        pidx_v[pl.ds(at, 1), :] = pencil
        code_ref[pl.ds(at, 1), :] = code
    to_scalar = pltpu.make_async_copy(pidx_v, pidx, own_sem.at[4])

    def phases(i, carry):
        code = code_ref[pl.ds(i, 1), :]
        mirror = code >= p.code_rows
        kx = jnp.where(mirror, code - p.code_rows, code)
        span = lax.broadcasted_iota(i32, (p.code_rows, LANE), 0)
        hot = jnp.where((span == kx) | ((span == p.gx) & mirror), 1.0, 0.0).astype(bf16)
        phase = lax.dot_general(hot, xt_ref[...], (((0,), (0,)), ((), ())), preferred_element_type=f32)
        phase_ref[pl.ds(pl.multiple_of(i * LANE, LANE), LANE), :] = phase.astype(bf16)
        return carry

    groups = p.gy // p.group // p.steps

    def z_step(q, carry):
        lanes = pl.ds(pl.multiple_of(q * p.group_lanes, LANE), p.group_lanes)
        v = v_ref[:, :, lanes].astype(f32)
        c = c_ref[:, :, lanes].astype(f32)
        parts = [v[i] * c[j] for i in range(p.nv) for j in range(p.nc)]
        if p.lanes_pad > p.lanes:
            parts.append(jnp.zeros((p.lanes_pad - p.lanes, p.group_lanes), f32))
        prod = jnp.concatenate(parts, axis=0).astype(bf16)
        for t_ref, (start, width, ys) in zip(zt_refs, p.windows()):
            z = lax.dot_general(
                t_ref[...],
                prod[:, start : start + width],
                (((1,), (1,)), ((), ())),
                preferred_element_type=f32,
            )
            for j in range(p.chunks):
                for i, y in enumerate(ys):
                    base = (q * p.group + y) * p.zpitch
                    z_ref[j, pl.ds(base, p.zrows), :] = z[i * p.zrows : (i + 1) * p.zrows, j * LANE : (j + 1) * LANE]
        return carry

    halves_all = (p.dests + 1) * p.halves
    for step in range(p.steps + 1):
        if step < p.steps:
            lax.fori_loop(halves_all * step // p.steps, halves_all * (step + 1) // p.steps, phases, 0)
            if step == 0:
                to_scalar.start()
            for d in range(1, far):
                for way in ways(d, step):
                    arrives(way, d, step).wait_recv()
                for way in ways(d + 1, step):
                    hop(way, d, step).start()
        if step > 0:
            if step == 1:
                for copy in local[:2]:
                    copy.wait()
            for way in ways(far, step - 1):
                arrives(way, far, step - 1).wait_recv()
            for d in range(1, p.inner):
                v_copy(d, step - 1).wait_recv()
            lax.fori_loop(groups * (step - 1), groups * step, z_step, 0)
    to_scalar.wait()

    def y_step(kz, carry):
        cols = []
        for j in range(p.chunks):
            parts = [z_ref[j, pl.ds(r * p.half + kz, p.gy, stride=p.zpitch), :] for r in range(2)]
            cols.append(jnp.concatenate(parts, axis=0).astype(bf16))
        rhs = jnp.concatenate(cols, axis=1)
        out = jnp.dot(yt_ref[...], rhs, preferred_element_type=f32)
        for s in range(2):
            for j in range(p.chunks):
                to = pl.ds(kz * (p.gy * p.pitch) + s * p.chunks + j, p.gy, stride=p.pitch)
                planes_ref[to, :] = out[s * p.gy : (s + 1) * p.gy, j * LANE : (j + 1) * LANE]
        return carry

    lax.fori_loop(0, p.half, y_step, 0)

    def number(i):
        if isinstance(i, int):
            return p.dests if i == 0 else lax.rem(me + i, p.dests)
        return jnp.where(i == 0, p.dests, lax.rem(me + i, p.dests))

    def pick(i, buf):
        at = number(i) * p.halves
        for g in range(p.rows_dest):
            src = pidx[at + g // LANE, g % LANE]
            buf[pl.ds(g * p.pitch, p.tile), :] = planes_ref[pl.ds(src, p.tile), :]

    def turn(i, buf):
        d = number(i)
        rows = pl.ds(pl.multiple_of(d * p.rows_dest, LANE), p.rows_dest)
        real, imag = [], []
        for j in range(p.chunks):
            re = buf[pl.ds(j, p.rows_dest, stride=p.pitch), :]
            im = buf[pl.ds(p.chunks + j, p.rows_dest, stride=p.pitch), :]
            cos = phase_ref[rows, j * LANE : (j + 1) * LANE].astype(f32)
            sin = phase_ref[rows, p.lanes_pad + j * LANE : p.lanes_pad + (j + 1) * LANE].astype(f32)
            real.append((cos * re - sin * im).astype(bf16))
            imag.append((sin * re + cos * im).astype(bf16))
        turned = jnp.concatenate(real + imag, axis=1)
        folded = jnp.dot(turned, fold_ref[...], preferred_element_type=f32)
        folded = folded * phase_ref[rows, 2 * p.lanes_pad :].astype(f32)
        total = folded[: p.rows_packed]
        for q in range(1, p.pack):
            total = total + pltpu.roll(folded[q * p.rows_packed : (q + 1) * p.rows_packed], q * 2 * p.pairs, 1)
        part_ref[d] = total.astype(bf16)

    def row_copy(k):
        to = lax.rem(me + k, p.dests)
        return remote(part_ref.at[to], row_ref.at[me], row_sem.at[0, k], row_sem.at[1, k], device(to))

    def block_copy(k):
        to = lax.rem(me + k, p.dests)
        src = part_ref.at[p.dests, pl.ds(0, p.block_rows)]
        return remote(src, block_ref.at[me], block_sem.at[0, k], block_sem.at[1, k], device(to))

    def send(k):
        @pl.when(k > 0)
        def _():
            row_copy(k).start()
            block_copy(k).start()

    pick(0, pick_a)

    def walk(j, carry):
        pick(2 * j + 1, pick_b)
        turn(2 * j, pick_a)
        send(2 * j - 1)
        pick(2 * j + 2, pick_a)
        turn(2 * j + 1, pick_b)
        send(2 * j)
        return carry

    lax.fori_loop(0, p.dests // 2, walk, 0)
    send(p.dests - 1)
    turn(p.dests, pick_a)
    row_ref[pl.ds(me, 1)] = part_ref[pl.ds(me, 1)]
    block_ref[pl.ds(me, 1)] = part_ref[p.dests :, : p.block_rows]

    for step in range(p.steps):
        for d in range(far):
            for way in ways(d + 1, step):
                hop(way, d, step).wait_send()
        for d in range(1, p.inner):
            v_copy(d, step).wait_send()

    def finish(k, carry):
        row_copy(k).wait()
        block_copy(k).wait()
        return carry

    lax.fori_loop(1, p.dests, finish, 0)

    def added(ref, b):
        total = ref[b].astype(f32)
        for k in range(1, p.cols):
            total = total + ref[k * p.bands + b].astype(f32)
        return total.astype(bf16)

    pair_lane = lax.broadcasted_iota(i32, (1, LANE), 1)
    group_lanes = 2 * p.pairs
    acc = [jnp.zeros((p.rows_packed, 2 * p.freqs * p.blocks), f32) for _ in range(p.pack)]
    for b in range(p.bands):
        rows = added(row_ref, b)
        block = added(block_ref, b).astype(f32)[: p.blocks]
        first = jnp.where(pair_lane < group_lanes, block, 0.0)
        turned = jnp.where(
            pair_lane < p.pairs,
            -pltpu.roll(first, LANE - p.pairs, 1),
            jnp.where(pair_lane < group_lanes, pltpu.roll(first, p.pairs, 1), 0.0),
        )
        parts = []
        for w in range(p.freqs):
            weight = weight_ref[b, w : w + 1, :]
            parts += [weight * first, weight * turned]
        right = jnp.concatenate(parts, axis=0)
        for q in range(p.pack):
            shifted = (pltpu.roll(right, q * group_lanes, 1) if q else right).astype(bf16)
            acc[q] = acc[q] + lax.dot_general(
                rows, shifted, (((1,), (1,)), ((), ())), preferred_element_type=f32
            )
    for q in range(p.pack):
        chi_ref[q * p.rows_packed : (q + 1) * p.rows_packed, :] = acc[q]


def run(p, v, c, cells, weights):
    tables = p.z_tables() + [p.y_table(), p.fold_table()]
    vmem, hbm = pl.BlockSpec(memory_space=pltpu.VMEM), pl.BlockSpec(memory_space=pl.ANY)
    dma = pltpu.SemaphoreType.DMA
    f32, bf16, i32 = jnp.float32, jnp.bfloat16, jnp.int32
    halves_all = (p.dests + 1) * p.halves
    return pl.pallas_call(
        functools.partial(kernel, p),
        out_shape=jax.ShapeDtypeStruct((p.rows_dest, 2 * p.freqs * p.blocks), f32),
        in_specs=[hbm] * 4 + [vmem] * (1 + len(tables)),
        out_specs=vmem,
        scratch_shapes=[
            pltpu.VMEM((p.chunks, (p.gy + 1) * p.zpitch, LANE), f32),
            pltpu.VMEM(((p.half * p.gy + 1) * p.pitch, LANE), f32),
            pltpu.VMEM(((p.rows_dest + 1) * p.pitch, LANE), f32),
            pltpu.VMEM(((p.rows_dest + 1) * p.pitch, LANE), f32),
            pltpu.VMEM((p.nv, p.slab_x, p.gy * p.gz), bf16),
            pltpu.VMEM((p.nc, p.slab_x, p.gy * p.gz), bf16),
            pltpu.VMEM((p.cols,) + cells.shape, i32),
            pltpu.VMEM((halves_all, LANE), i32),
            pltpu.SMEM((halves_all, LANE), i32),
            pltpu.VMEM((halves_all, LANE), i32),
            pltpu.VMEM((halves_all * LANE, p.wide), bf16),
            pltpu.VMEM((p.code_rows, p.wide), bf16),
            pltpu.VMEM((p.dests + 1, p.rows_packed, LANE), bf16),
            pltpu.VMEM((p.dests, p.rows_packed, LANE), bf16),
            pltpu.VMEM((p.dests, p.block_rows, LANE), bf16),
            dma((5,)),
            dma((p.inner - 1, p.steps)),
            dma((p.inner - 1, p.steps)),
            dma((2, p.outer // 2, p.steps)),
            dma((2, p.outer // 2, p.steps)),
            dma((2, p.cols - 1)),
            dma((2, p.dests)),
            dma((2, p.dests)),
        ],
        compiler_params=pltpu.CompilerParams(
            collective_id=0, has_side_effects=True, vmem_limit_bytes=VMEM_LIMIT
        ),
        name="chi",
    )(v, c, cells, p.x_tables(), weights, *tables)


def pair_weights(p, valence_index, occupied_energy, conduction_energy, frequency):
    span = jnp.arange(occupied_energy.shape[0], dtype=jnp.int32)
    hit = valence_index[:, None] == span[None, :]
    valence_energy = jnp.sum(jnp.where(hit, occupied_energy[None, :], 0.0), axis=1)
    gap = conduction_energy[None, :] - valence_energy[:, None]
    freq = frequency[:, None, None]
    norm = 1.0 / math.sqrt(gap.size)
    weights = -4.0 * gap[None] / (gap[None] * gap[None] + freq * freq) * norm
    split = weights.reshape(-1, p.outer, p.nv, p.outer, p.inner, p.c_own)
    split = split.transpose(1, 4, 0, 2, 3, 5).reshape(p.bands, -1, p.pairs)
    return jnp.tile(split, (1, 1, LANE // p.pairs))


def per_device(
    valence_wave,
    conduction_wave,
    valence_index,
    occupied_energy,
    conduction_energy,
    frequency,
    gvec_cell,
    block_cell,
):
    cols, bands = lax.axis_size("col"), lax.axis_size("band")
    p = Plan(
        valence_wave.shape[0],
        conduction_wave.shape[0],
        valence_wave.shape[1],
        valence_wave.shape[2],
        cols,
        bands,
        gvec_cell.shape[0] * cols,
        block_cell.shape[0] * cols,
        frequency.shape[0],
    )
    weights = pair_weights(p, valence_index, occupied_energy, conduction_energy, frequency)
    tail = jnp.pad(block_cell, (0, SUB * LANE - block_cell.shape[0]))
    cells = jnp.concatenate([gvec_cell, tail]).reshape(-1, LANE)
    return run(p, valence_wave, conduction_wave, cells, weights)


def solution(mesh):
    return jax.shard_map(
        per_device,
        mesh=mesh,
        in_specs=(
            P("band", "col", None),
            P("band", "col", None),
            P(),
            P(),
            P(),
            P(),
            P("col"),
            P("col"),
        ),
        out_specs=P(("col", "band"), None),
        check_vma=False,
    )
```

time: 294 us -> 90.2 us (0.31)
  matrix products: 96 us -> 0 us
  blocking collectives: 85.4 us -> 0 us
  Pallas kernels: 0 us -> 85 us
  waiting for transfers between devices: 43.3 us -> 0 us
  local copies, waits for them, and re-layouts: 32.5 us -> 3.23 us
  other arithmetic: 18.3 us -> 1.73 us
  between operations: 14.3 us -> 0.04 us
  starting transfers between devices: 3.33 us -> 0 us
    dot_general x11 -> x0, matrix products: 96 us -> none  [the longest x2 42.4 us: partial_density(): jnp.einsum('ogc,socn->sogn', one_hot(cells % slab, slab), planes, preferr...]
    pallas_call x0 -> x1, Pallas kernels: none -> 85 us  [run(): pl.pallas_call(functools.partial(kernel, p), out_shape=jax.ShapeDtypeStru...]
    all_gather x2 -> x0, blocking collectives: 79.1 us -> none  [the longest x1 73.7 us: per_device(): lax.all_gather(block_part, both, axis=0)]
    all_gather x1 -> x0, waiting for transfers between devices: 42.6 us -> none  [per_device(): conduction_all = lax.all_gather(conduction_wave, 'band', axis=0, tiled=True)]
    convert_element_type x3 -> x0, local copies, waits for them, and re-layouts: 15.3 us -> none  [the longest x1 15.2 us: per_device(): jnp.einsum('srjy,rkyn->sjkn', y_table, z_done, preferred_element_type=f32)]
    convert_element_type x8 -> x0, other arithmetic: 15.2 us -> none  [the longest x1 7.14 us: per_device(): (valence_wave.astype(f32)[:, None] * conduction_all.astype(f32)[None]).as...]
    transpose x3 -> x0, local copies, waits for them, and re-layouts: 11.4 us -> none  [the longest x1 10.3 us: per_device(): products.reshape(lanes, plane_size).T.reshape(grid_y, grid_z, lanes)]
    unnamed x1 -> x0, blocking collectives: 6.38 us -> none
  transfers between devices with their start and end apart: 2 -> 0, of which waited for: 1 -> 0; matrix products, arithmetic and copies ran while one was open for 5% -> 0% of each run, Pallas kernels for 0% -> 0%
where the time goes in v2:
time: 90.2 us; the launch traced here: 90 us
  Pallas kernels  85 us (94%)
  local copies, waits for them, and re-layouts  3.23 us (4%)
  other arithmetic  1.73 us (2%)
    pallas_call x1, Pallas kernels, run(): pl.pallas_call(functools.partial(kernel, p), out_shape=jax.ShapeDtypeStru...  85 us
    unnamed x9, local copies, waits for them, and re-layouts  2.14 us

profile of v2, /device:TPU:0, one launch (start us, length us, event | category | flops | bytes accessed | tf_op | source)
XLA Modules:
  0.0 90.0 jit_solution(6128907361284648230)
XLA Ops:
  0.0 0.0 copy-start.3
  0.0 0.0 copy-start.1
  0.0 1.0 %select_reduce_fusion = f32[16]{0:T(128)S(1)} fusion(f32[4096]{0:T(1024)} %param.16, s32[16]{0:T(128)} %param.15), kind=kLoop, calls=%fused_computation | loop fusion | flops 196592 | bytes 16512 | tf_op jit(solution)/shard_map/reduce_sum | solution.py:462
  1.0 0.0 copy-done.3
  1.0 0.0 copy-start
  1.0 0.1 sub.26
  1.1 0.0 copy-done.1
  1.1 0.1 sub.24
  1.2 0.0 copy-start.2
  1.2 0.1 copy.16
  1.3 0.4 copy-done
  1.7 0.2 copy-done.2
  1.8 0.6 fusion.cell_in
  2.4 0.1 subtract_multiply_fusion.1
  2.5 0.1 multiply_bitcast_fusion
  2.6 0.1 tile.10
  2.7 0.7 tile.12.weight_ref
  3.4 85.0 %chi.1 = f32[256,128]{1,0:T(8,128)} custom-call(bf16[2,24,9216]{2,1,0:T(8,128)(2,1)} %v_in.1, bf16[1,24,9216]{2,1,0:T(8,128)(2,1)} %c_in.1, s32[24,128]{1,0:T(8,128)} %fusion.cell_in, bf16[4,128,896]{2,1,0:T(8,128)(2,1)} %constant.22.clone.xt_in, f32[8,4,128]{2,1,0:T(4,128)} %tile.12.weight_ref, bf16[208,256]{1,0:T(8,128)(2,1)} %constant.18.clone.refs_0_, ...), custom_call_target="tpu_custom_call" | custom-call | tf_op jit(solution)/shard_map/chi/pallas_call | solution.py:422
  88.4 1.6 %copy.18 = f32[256,128]{1,0:T(8,128)} copy(f32[256,128]{1,0:T(8,128)} %chi.1) | data formatting | bytes 262144
  (2 shorter events, 0.0 us)
Async XLA Ops:
  0.0 1.0 %copy-start.3 = (f32[4]{0:T(128)S(1)}, f32[4]{0:T(128)}, u32[]{:S(2)}) copy-start(f32[4]{0:T(128)} %param.18) | copy-start | bytes 52
  0.0 1.1 %copy-start.1 = (f32[8]{0:T(128)S(1)}, f32[8]{0:T(128)}, u32[]{:S(2)}) copy-start(f32[8]{0:T(128)} %param.17) | copy-start | bytes 100
  1.0 0.7 copy-start
  1.2 0.7 copy-start.2

commit v3 on v2

v3 whole, which is shorter than its diff:
```python
import functools
import math

import jax
import jax.numpy as jnp
import numpy as np
from jax import lax
from jax.experimental import pallas as pl
from jax.experimental.pallas import tpu as pltpu
from jax.sharding import PartitionSpec as P

GY = 96
LANE = 128
SUB = 8
INNER = 2
STEPS = 6
UNROLL_PHASE = 4
UNROLL_Y = 7
UNROLL_Z = 2
MESH = pl.DeviceIdType.MESH
VMEM_LIMIT = 66_000_000


def up(n, k):
    return -(-n // k) * k


def rounded(a):
    return jnp.asarray(a, jnp.bfloat16)


def angles(rows, cols, length):
    return 2.0 * math.pi * ((np.outer(rows, cols) % length) / length)


class Plan:
    def __init__(self, v_own, c_own, slab_x, plane, cols, bands, rows_all, blocks_all, freqs):
        self.inner = INNER if bands % INNER == 0 else 1
        self.outer = bands // self.inner
        self.v_own, self.c_own = v_own, c_own
        self.nv, self.nc, self.slab_x = v_own * self.inner, c_own * self.outer, slab_x
        self.gy, self.gz, self.gx = GY, plane // GY, slab_x * cols
        self.cols, self.bands, self.freqs = cols, bands, freqs
        self.pairs = self.nv * self.nc
        self.merge = max(1, min(self.outer, LANE // (c_own * self.nv * slab_x)))
        if self.outer % self.merge:
            self.merge = 1
        self.chunks = self.outer // self.merge
        self.chunk_pairs = self.pairs // self.chunks
        self.lanes = self.chunk_pairs * slab_x
        self.tile = up(2 * self.chunks, SUB)
        self.pitch = self.tile + 1
        self.half = self.gz // 2 + 1
        self.zrows = up(2 * self.half, SUB)
        self.zpitch = self.zrows + 1
        self.group_lanes = self.gz * LANE // math.gcd(self.gz, LANE)
        self.group = self.group_lanes // self.gz
        self.dests = cols * bands
        self.rows_dest = rows_all // self.dests
        self.halves = self.rows_dest // LANE
        self.pack = LANE // (2 * self.pairs)
        self.rows_packed = self.rows_dest // self.pack
        self.cell_rows = rows_all // cols // LANE
        self.blocks = blocks_all
        self.block_rows = up(blocks_all, 2 * SUB)
        self.steps = STEPS
        self.code_rows = up(self.gx + 1, LANE)
        self.wide = 3 * LANE
        self.valences, self.conductions = v_own * bands, c_own * bands

    def stages(self):
        if self.merge > 1:
            return [list(range(self.chunks))]
        return [list(range(k, min(k + 2, self.chunks))) for k in range(0, self.chunks, 2)]

    def arrivals(self, at):
        return sorted(range(self.outer), key=lambda o: (abs(o - at), o))

    def windows(self):
        out, y = [], 0
        while y < self.group:
            start = y * self.gz // LANE * LANE
            ys = []
            while y < self.group and (y + 1) * self.gz <= start + 2 * LANE:
                ys.append(y)
                y += 1
            width = up(ys[-1] * self.gz + self.gz - start, LANE)
            out.append((start, width, ys))
        return out

    def z_tables(self):
        ang = angles(np.arange(self.half), np.arange(self.gz), self.gz)
        one = np.zeros((self.zrows, self.gz), np.float32)
        one[: self.half] = np.cos(ang)
        one[self.half : 2 * self.half] = -np.sin(ang)
        tables = []
        for start, width, ys in self.windows():
            t = np.zeros((len(ys) * self.zrows, width), np.float32)
            for i, y in enumerate(ys):
                lo = y * self.gz - start
                t[i * self.zrows : (i + 1) * self.zrows, lo : lo + self.gz] = one
            tables.append(rounded(t))
        return tables

    def y_table(self):
        ang = angles(np.arange(self.gy), np.arange(self.gy), self.gy)
        scale = 1.0 / math.sqrt(self.gy * self.gz)
        cos, sin = np.cos(ang) * scale, -np.sin(ang) * scale
        return rounded(np.block([[cos, -sin], [sin, cos]]))

    def x_tables(self):
        out = np.zeros((self.cols, self.code_rows, self.wide), np.float32)
        out[:, : self.gx, 2 * LANE :] = 1.0
        out[:, self.gx, 2 * LANE + self.pairs :] = -2.0
        scale = 1.0 / math.sqrt(self.gx)
        for col in range(self.cols):
            xs = col * self.slab_x + np.arange(self.lanes) % self.slab_x
            ang = angles(np.arange(self.gx), xs, self.gx)
            out[col, : self.gx, : self.lanes] = np.cos(ang) * scale
            out[col, : self.gx, LANE : LANE + self.lanes] = -np.sin(ang) * scale
        return rounded(out)

    def fold_table(self):
        out = np.zeros((2 * LANE, LANE), np.float32)
        n = np.arange(self.lanes)
        out[n, n // self.slab_x] = 1.0
        out[LANE + n, self.pairs + n // self.slab_x] = 1.0
        return rounded(out)


def place(p):
    band = lax.axis_index("band")
    return band // p.inner, lax.rem(band, p.inner)


def remote(src, dst, send, recv, target):
    return pltpu.make_async_remote_copy(src, dst, send, recv, device_id=target, device_id_type=MESH)


def kernel(p, index_in, energy_in, conduction_in, freq_in, v_in, c_in, cell_in, block_in, xt_in, *refs):
    n_win = len(p.windows())
    zt_refs = refs[:n_win]
    (yt_ref, fold_ref, chi_ref, z_ref, planes_ref, pick_a, pick_b, v_ref, c_ref, cells, blocks_v, blocks, pidx_v, pidx, code_ref,
     phase_ref, xt_ref, part_ref, row1, sum_ref, row_ref, block1, block_ref, own_sem, vs, vr, cs, cr, cell_sem, sem1, sem2, met) = refs[n_win:]
    f32, bf16, i32 = jnp.float32, jnp.bfloat16, jnp.int32
    outer, inner = place(p)
    col, band = lax.axis_index("col"), lax.axis_index("band")
    line = [(outer > 0, outer - 1), (outer < p.outer - 1, outer + 1)]
    near = [(band, lax.rem(col + d, p.cols)) for d in range(1, p.cols)]
    near += [(outer * p.inner + lax.rem(inner + d, p.inner), col) for d in range(1, p.inner)]
    greeted = len(near) + sum(jnp.where(there, 1, 0) for there, _ in line)

    barrier = pltpu.get_barrier_semaphore()
    for target in near:
        pl.semaphore_signal(barrier, inc=1, device_id=target, device_id_type=MESH)
    for there, o in line:

        @pl.when(there)
        def _():
            pl.semaphore_signal(barrier, inc=1, device_id=(o * p.inner + inner, col), device_id_type=MESH)

    local = [
        pltpu.make_async_copy(v_in, v_ref.at[pl.ds(inner * p.v_own, p.v_own)], own_sem.at[0]),
        pltpu.make_async_copy(c_in, c_ref.at[pl.ds(outer * p.c_own, p.c_own)], own_sem.at[1]),
        pltpu.make_async_copy(cell_in, cells.at[col], own_sem.at[2]),
        pltpu.make_async_copy(xt_in.at[col], xt_ref, own_sem.at[3]),
        pltpu.make_async_copy(block_in, blocks_v.at[col], own_sem.at[4]),
    ]
    for copy in local:
        copy.start()
    pl.semaphore_wait(barrier, greeted)

    step_lanes = p.gy * p.gz // p.steps

    def cut(ref, step):
        return ref.at[:, :, pl.ds(step * step_lanes, step_lanes)]

    def v_copy(d, step):
        slot = v_ref.at[pl.ds(inner * p.v_own, p.v_own)]
        target = (outer * p.inner + lax.rem(inner + d, p.inner), col)
        return remote(cut(v_in, step), cut(slot, step), vs.at[d - 1, step], vr.at[d - 1, step], target)

    def hop(way, d, step):
        slot = c_ref.at[pl.ds((outer - d if way == 0 else outer + d) * p.c_own, p.c_own)]
        target = ((outer + (1 if way == 0 else -1)) * p.inner + inner, col)
        src = c_in if d == 0 else slot
        return remote(cut(src, step), cut(slot, step), cs.at[way, d, step], cr.at[way, d, step], target)

    def arrives(way, d, step):
        slot = c_ref.at[pl.ds((outer - d if way == 0 else outer + d) * p.c_own, p.c_own)]
        return remote(cut(slot, step), cut(slot, step), cs.at[way, d - 1, step], cr.at[way, d - 1, step], (band, col))

    def passes(way, d):
        if way == 0:
            return (outer >= d) & (outer < p.outer - 1)
        return (outer + d < p.outer) & (outer > 0)

    def pass_on(d, step):
        for way in range(2):

            @pl.when(passes(way, d))
            def _():
                if d > 0:
                    arrives(way, d, step).wait_recv()
                hop(way, d, step).start()

    def wait_ends(d, step):
        @pl.when(outer == p.outer - 1)
        def _():
            arrives(0, d, step).wait_recv()

        @pl.when(outer == 0)
        def _():
            arrives(1, d, step).wait_recv()

    cell_copies = []
    for d in range(1, p.cols):
        target = (band, lax.rem(col + d, p.cols))
        cell_copies.append(remote(cell_in, cells.at[col], cell_sem.at[0, 0, d - 1], cell_sem.at[1, 0, d - 1], target))
        cell_copies.append(remote(block_in, blocks_v.at[col], cell_sem.at[0, 1, d - 1], cell_sem.at[1, 1, d - 1], target))
    for copy in cell_copies:
        copy.start()
    for step in range(p.steps):
        pass_on(0, step)
        for d in range(1, p.inner):
            v_copy(d, step).start()

    for copy in local[2:]:
        copy.wait()
    for copy in cell_copies:
        copy.wait()
    to_scalar = pltpu.make_async_copy(blocks_v, blocks, own_sem.at[5])
    to_scalar.start()
    slab_y = p.gy // p.cols

    def points(values, owner):
        def split(a, n):
            high = lax.div(a, jnp.full(a.shape, n, i32))
            return high, a - high * n

        kx, rest = split(values, slab_y * p.gz)
        ky, kz = split(rest, p.gz)
        ky = ky + owner * slab_y
        mirror = kz >= p.half
        kx = jnp.where(mirror & (kx > 0), p.gx - kx, kx)
        ky = jnp.where(mirror & (ky > 0), p.gy - ky, ky)
        kz = jnp.where(mirror, p.gz - kz, kz)
        return (kz * p.gy + ky) * p.pitch, kx + jnp.where(mirror, p.code_rows, 0)

    for k in range(p.cols):
        rows = pl.ds(k * p.cell_rows, p.cell_rows)
        pidx_v[rows, :], code_ref[rows, :] = points(cells[k], k)
    last = jnp.zeros((1, LANE), i32)
    lane_owner = jnp.zeros((1, LANE), i32)
    lane = lax.broadcasted_iota(i32, (1, LANE), 1)
    per_owner = p.blocks // p.cols
    to_scalar.wait()
    for k in range(p.cols):
        for m in range(per_owner):
            here = lane == k * per_owner + m
            last = jnp.where(here, blocks[k, 0, m], last)
            lane_owner = jnp.where(here, k, lane_owner)
    pencil, code = points(last, lane_owner)
    for k in range(p.halves):
        at = p.dests * p.halves + k
        pidx_v[pl.ds(at, 1), :] = pencil
        code_ref[pl.ds(at, 1), :] = code
    to_scalar = pltpu.make_async_copy(pidx_v, pidx, own_sem.at[6])

    def phases(i, carry):
        code = code_ref[pl.ds(i, 1), :]
        mirror = code >= p.code_rows
        kx = jnp.where(mirror, code - p.code_rows, code)
        span = lax.broadcasted_iota(i32, (p.code_rows, LANE), 0)
        hot = jnp.where((span == kx) | ((span == p.gx) & mirror), 1.0, 0.0).astype(bf16)
        phase = lax.dot_general(hot, xt_ref[...], (((0,), (0,)), ((), ())), preferred_element_type=f32)
        phase_ref[pl.ds(pl.multiple_of(i * LANE, LANE), LANE), :] = phase.astype(bf16)
        return carry

    groups = p.gy // p.group // p.steps

    def by_place(values):
        out = values[0]
        for o in range(1, p.outer):
            out = jnp.where(outer == o, values[o], out)
        return out

    order = [by_place([p.arrivals(o)[k] for o in range(p.outer)]) for k in range(p.outer)]

    def chunk(k):
        return k if p.merge > 1 else order[k]

    def z_step(stage, q, carry):
        lanes = pl.ds(pl.multiple_of(q * p.group_lanes, LANE), p.group_lanes)
        v = v_ref[:, :, lanes].astype(f32)
        parts = []
        for k in stage:
            size = p.merge * p.c_own
            c = c_ref[pl.ds(chunk(k) * size, size), :, lanes].astype(f32)
            parts += [v[i] * c[j] for j in range(size) for i in range(p.nv)]
            if LANE > p.lanes:
                parts.append(jnp.zeros((LANE - p.lanes, p.group_lanes), f32))
        prod = jnp.concatenate(parts, axis=0).astype(bf16)
        for t_ref, (start, width, ys) in zip(zt_refs, p.windows()):
            z = lax.dot_general(
                t_ref[...],
                prod[:, start : start + width],
                (((1,), (1,)), ((), ())),
                preferred_element_type=f32,
            )
            for n, k in enumerate(stage):
                for i, y in enumerate(ys):
                    base = (q * p.group + y) * p.zpitch
                    z_ref[chunk(k), pl.ds(base, p.zrows), :] = z[i * p.zrows : (i + 1) * p.zrows, n * LANE : (n + 1) * LANE]
        return carry

    def y_step(stage, kz, carry):
        cols = []
        for k in stage:
            parts = [z_ref[chunk(k), pl.ds(r * p.half + kz, p.gy, stride=p.zpitch), :] for r in range(2)]
            cols.append(jnp.concatenate(parts, axis=0).astype(bf16))
        out = jnp.dot(yt_ref[...], jnp.concatenate(cols, axis=1), preferred_element_type=f32)
        for s in range(2):
            for n, k in enumerate(stage):
                to = pl.ds(kz * (p.gy * p.pitch) + s * p.chunks + chunk(k), p.gy, stride=p.pitch)
                planes_ref[to, :] = out[s * p.gy : (s + 1) * p.gy, n * LANE : (n + 1) * LANE]
        return carry

    groups = p.gy // p.group // p.steps
    halves_all = (p.dests + 1) * p.halves
    stages = p.stages()
    cuts = [s[-1] + 1 if p.merge == 1 else p.outer for s in stages]

    def share(n, part, parts):
        return n * part // parts, n * (part + 1) // parts

    def looped(low, high, body, unroll):
        trips = (high - low) // unroll

        def several(i, carry):
            for u in range(unroll):
                body(low + i * unroll + u, carry)
            return carry

        if trips > 0:
            lax.fori_loop(0, trips, several, 0)
        for i in range(low + trips * unroll, high):
            body(i, 0)

    passed = 1
    for t, stage in enumerate(stages):
        until = p.outer - 1 if t == len(stages) - 1 else passed + 1
        for step in range(p.steps):
            if t == 0:
                looped(*share(halves_all, step, p.steps), phases, UNROLL_PHASE)
                if step == 0:
                    to_scalar.start()
            else:
                looped(*share(p.half, step, p.steps), functools.partial(y_step, stages[t - 1]), UNROLL_Y)
            for d in range(passed, until):
                pass_on(d, step)
            if t == 0:
                if step == 0:
                    for copy in local[:2]:
                        copy.wait()
                for d in range(1, p.inner):
                    v_copy(d, step).wait_recv()
            for d in range(max(1, cuts[t - 1] if t else 1), cuts[t]):
                wait_ends(d, step)
            looped(groups * step, groups * (step + 1), functools.partial(z_step, stage), UNROLL_Z)
        passed = until
    for d in range(1, p.inner):
        target = (outer * p.inner + lax.rem(inner + d, p.inner), col)
        pl.semaphore_signal(met, inc=1, device_id=target, device_id_type=MESH)
    to_scalar.wait()
    looped(0, p.half, functools.partial(y_step, stages[-1]), UNROLL_Y)
    if p.inner > 1:
        pl.semaphore_wait(met, p.inner - 1)

    def target_band(t):
        back = p.bands - 1 - t
        o = lax.rem(outer + lax.div(back, p.inner), p.outer)
        return o * p.inner + lax.rem(inner + lax.rem(back, p.inner), p.inner)

    def number(t, c):
        return lax.rem(col + 1 + c, p.cols) * p.bands + target_band(t)

    def pick(d, buf):
        at = d * p.halves
        for g in range(p.rows_dest):
            src = pidx[at + g // LANE, g % LANE]
            buf[pl.ds(g * p.pitch, p.tile), :] = planes_ref[pl.ds(src, p.tile), :]

    def turn(d, buf):
        rows = pl.ds(pl.multiple_of(d * p.rows_dest, LANE), p.rows_dest)
        cos = phase_ref[rows, :LANE].astype(f32)
        sin = phase_ref[rows, LANE : 2 * LANE].astype(f32)
        folded = 0.0
        for j in range(p.chunks):
            re = buf[pl.ds(j, p.rows_dest, stride=p.pitch), :]
            im = buf[pl.ds(p.chunks + j, p.rows_dest, stride=p.pitch), :]
            turned = jnp.concatenate([(cos * re - sin * im).astype(bf16), (sin * re + cos * im).astype(bf16)], axis=1)
            part = jnp.dot(turned, fold_ref[...], preferred_element_type=f32)
            folded = folded + (pltpu.roll(part, j * p.chunk_pairs, 1) if j else part)
        folded = folded * phase_ref[rows, 2 * LANE :].astype(f32)
        total = folded[: p.rows_packed]
        for q in range(1, p.pack):
            total = total + pltpu.roll(folded[q * p.rows_packed : (q + 1) * p.rows_packed], q * 2 * p.pairs, 1)
        part_ref[d] = total.astype(bf16)

    def peer(c):
        return (band, lax.rem(col + 1 + c, p.cols))

    def part_copy(t, c):
        return remote(part_ref.at[number(t, c)], row1.at[c, t], sem1.at[0, c, t], sem1.at[1, c, t], peer(c))

    def block_part_copy(c):
        src = part_ref.at[p.dests, pl.ds(0, p.block_rows)]
        return remote(src, block1.at[c], sem1.at[0, c, p.bands], sem1.at[1, c, p.bands], peer(c))

    def sum_copies(t):
        target = (target_band(t), col)
        return (
            remote(sum_ref.at[t], row_ref.at[band], sem2.at[0, 0, t], sem2.at[1, 0, t], target),
            remote(
                sum_ref.at[p.bands, pl.ds(0, p.block_rows)],
                block_ref.at[band],
                sem2.at[0, 1, t],
                sem2.at[1, 1, t],
                target,
            ),
        )

    def add_up(t):
        total = part_ref[number(t, p.cols - 1)].astype(f32)
        for c in range(p.cols - 1):
            part_copy(t, c).wait_recv()
        for c in range(p.cols - 1):
            total = total + row1[c, t].astype(f32)
        return total.astype(bf16)

    def add_up_block():
        total = part_ref[p.dests, : p.block_rows, :].astype(f32)
        for c in range(p.cols - 1):
            block_part_copy(c).wait_recv()
        for c in range(p.cols - 1):
            total = total + block1[c].astype(f32)
        return total.astype(bf16)

    def when(condition, action):
        pl.when(condition)(action)

    buffers = (pick_a, pick_b)
    pick(p.dests, pick_a)

    def send_sums(t):
        for copy in sum_copies(t):
            copy.start()

    def walk(t, carry):
        for c in range(p.cols):
            pick(number(t, c), buffers[(c + 1) % 2])
            if c == 0:
                turn(jnp.where(t == 0, p.dests, number(t - 1, p.cols - 1)), buffers[0])
                when(t > 0, lambda: part_copy(t - 1, p.cols - 2).start())
            else:
                turn(number(t, c - 1), buffers[c % 2])
                if c > 1:
                    part_copy(t, c - 2).start()
            if c == 1:
                when(t > 1, lambda: send_sums(t - 2))
            if c == min(2, p.cols - 1):

                @pl.when(t == 0)
                def _():
                    for k in range(p.cols - 1):
                        block_part_copy(k).start()

        @pl.when(t == 1)
        def _():
            sum_ref[p.bands, : p.block_rows, :] = add_up_block()

        @pl.when(t > 0)
        def _():
            sum_ref[t - 1] = add_up(t - 1)

        return carry

    lax.fori_loop(0, p.bands, walk, 0)
    last = p.bands - 1
    part_copy(last, p.cols - 2).start()
    turn(number(last, p.cols - 1), buffers[0])
    send_sums(last - 1)
    row_ref[band] = add_up(last)
    block_ref[band] = sum_ref[p.bands, : p.block_rows, :]

    for step in range(p.steps):
        for d in range(p.outer - 1):
            for way in range(2):

                @pl.when(passes(way, d))
                def _():
                    hop(way, d, step).wait_send()

        for d in range(1, p.inner):
            v_copy(d, step).wait_send()

    def close_parts(t, carry):
        for c in range(p.cols - 1):
            part_copy(t, c).wait_send()
        return carry

    lax.fori_loop(0, p.bands, close_parts, 0)
    for c in range(p.cols - 1):
        block_part_copy(c).wait_send()

    def close_sums(t, carry):
        for copy in sum_copies(t):
            copy.wait()
        return carry

    lax.fori_loop(0, p.bands - 1, close_sums, 0)

    pair_lane = lax.broadcasted_iota(i32, (1, LANE), 1)
    pair = lax.rem(pair_lane, p.pairs)
    pair_v, pair_c = lax.rem(pair, p.nv), lax.div(pair, p.nv)

    def spread(which, values):
        out = jnp.zeros((1, LANE), f32)
        for k, value in enumerate(values):
            out = jnp.where(which == k, value, out)
        return out

    valence = [energy_in[index_in[i]] for i in range(p.valences)]
    valence = [spread(pair_v, valence[o * p.nv : (o + 1) * p.nv]) for o in range(p.outer)]
    conduction = [
        spread(pair_c, [conduction_in[(o * p.inner + i) * p.c_own + l] for o in range(p.outer) for l in range(p.c_own)])
        for i in range(p.inner)
    ]
    norm = 1.0 / math.sqrt(p.valences * p.conductions)
    group_lanes = 2 * p.pairs
    acc = [jnp.zeros((p.rows_packed, 2 * p.freqs * p.blocks), f32) for _ in range(p.pack)]
    for b in range(p.bands):
        rows = row_ref[b]
        block = block_ref[b].astype(f32)[: p.blocks]
        first = jnp.where(pair_lane < group_lanes, block, 0.0)
        turned = jnp.where(
            pair_lane < p.pairs,
            -pltpu.roll(first, LANE - p.pairs, 1),
            jnp.where(pair_lane < group_lanes, pltpu.roll(first, p.pairs, 1), 0.0),
        )
        gap = conduction[b % p.inner] - valence[b // p.inner]
        parts = []
        for w in range(p.freqs):
            weight = -4.0 * gap / (gap * gap + freq_in[w] * freq_in[w]) * norm
            parts += [weight * first, weight * turned]
        right = jnp.concatenate(parts, axis=0)
        for q in range(p.pack):
            shifted = (pltpu.roll(right, q * group_lanes, 1) if q else right).astype(bf16)
            acc[q] = acc[q] + lax.dot_general(
                rows, shifted, (((1,), (1,)), ((), ())), preferred_element_type=f32
            )
    for q in range(p.pack):
        chi_ref[q * p.rows_packed : (q + 1) * p.rows_packed, :] = acc[q]


def run(p, index, energy, conduction, freq, v, c, cells, blocks):
    tables = p.z_tables() + [p.y_table(), p.fold_table()]
    vmem, hbm = pl.BlockSpec(memory_space=pltpu.VMEM), pl.BlockSpec(memory_space=pl.ANY)
    dma = pltpu.SemaphoreType.DMA
    f32, bf16, i32 = jnp.float32, jnp.bfloat16, jnp.int32
    halves_all = (p.dests + 1) * p.halves
    return pl.pallas_call(
        functools.partial(kernel, p),
        out_shape=jax.ShapeDtypeStruct((p.rows_dest, 2 * p.freqs * p.blocks), f32),
        in_specs=[pl.BlockSpec(memory_space=pltpu.SMEM)] * 4 + [hbm] * 5 + [vmem] * len(tables),
        out_specs=vmem,
        scratch_shapes=[
            pltpu.VMEM((p.chunks, (p.gy + 1) * p.zpitch, LANE), f32),
            pltpu.VMEM(((p.half * p.gy + 1) * p.pitch, LANE), f32),
            pltpu.VMEM(((p.rows_dest + 1) * p.pitch, LANE), f32),
            pltpu.VMEM(((p.rows_dest + 1) * p.pitch, LANE), f32),
            pltpu.VMEM((p.nv, p.slab_x, p.gy * p.gz), bf16),
            pltpu.VMEM((p.nc, p.slab_x, p.gy * p.gz), bf16),
            pltpu.VMEM((p.cols,) + cells.shape, i32),
            pltpu.VMEM((p.cols,) + blocks.shape, i32),
            pltpu.SMEM((p.cols,) + blocks.shape, i32),
            pltpu.VMEM((halves_all, LANE), i32),
            pltpu.SMEM((halves_all, LANE), i32),
            pltpu.VMEM((halves_all, LANE), i32),
            pltpu.VMEM((halves_all * LANE, p.wide), bf16),
            pltpu.VMEM((p.code_rows, p.wide), bf16),
            pltpu.VMEM((p.dests + 1, p.rows_packed, LANE), bf16),
            pltpu.VMEM((p.cols - 1, p.bands, p.rows_packed, LANE), bf16),
            pltpu.VMEM((p.bands + 1, p.rows_packed, LANE), bf16),
            pltpu.VMEM((p.bands, p.rows_packed, LANE), bf16),
            pltpu.VMEM((p.cols - 1, p.block_rows, LANE), bf16),
            pltpu.VMEM((p.bands, p.block_rows, LANE), bf16),
            dma((7,)),
            dma((p.inner - 1, p.steps)),
            dma((p.inner - 1, p.steps)),
            dma((2, p.outer - 1, p.steps)),
            dma((2, p.outer - 1, p.steps)),
            dma((2, 2, p.cols - 1)),
            dma((2, p.cols - 1, p.bands + 1)),
            dma((2, 2, p.bands)),
            pltpu.SemaphoreType.REGULAR,
        ],
        compiler_params=pltpu.CompilerParams(
            collective_id=0, has_side_effects=True, vmem_limit_bytes=VMEM_LIMIT
        ),
        name="chi",
    )(index, energy, conduction, freq, v, c, cells, blocks, p.x_tables(), *tables)


def per_device(
    valence_wave,
    conduction_wave,
    valence_index,
    occupied_energy,
    conduction_energy,
    frequency,
    gvec_cell,
    block_cell,
):
    cols, bands = lax.axis_size("col"), lax.axis_size("band")
    p = Plan(
        valence_wave.shape[0],
        conduction_wave.shape[0],
        valence_wave.shape[1],
        valence_wave.shape[2],
        cols,
        bands,
        gvec_cell.shape[0] * cols,
        block_cell.shape[0] * cols,
        frequency.shape[0],
    )
    return run(
        p,
        valence_index,
        occupied_energy,
        conduction_energy,
        frequency,
        valence_wave,
        conduction_wave,
        gvec_cell.reshape(-1, LANE),
        block_cell.reshape(1, -1),
    )


def solution(mesh):
    return jax.shard_map(
        per_device,
        mesh=mesh,
        in_specs=(
            P("band", "col", None),
            P("band", "col", None),
            P(),
            P(),
            P(),
            P(),
            P("col"),
            P("col"),
        ),
        out_specs=P(("col", "band"), None),
        check_vma=False,
    )
```

time: 90.2 us -> 70 us (0.78)
  Pallas kernels: 85 us -> 68.3 us
  other arithmetic: 1.73 us -> 0 us
  local copies, waits for them, and re-layouts: 3.23 us -> 1.57 us
    pallas_call x1, Pallas kernels: 85 us -> 68.3 us  [run(): pl.pallas_call(functools.partial(kernel, p), out_shape=jax.ShapeDtypeStru...]
    reduce_sum x1 -> x0, other arithmetic: 0.96 us -> none  [pair_weights(): jnp.sum(jnp.where(hit, occupied_energy[None, :], 0.0), axis=1)]
    unnamed x9 -> x1, local copies, waits for them, and re-layouts: 2.14 us -> 1.57 us
where the time goes in v3:
time: 70 us; the launch traced here: 69.8 us
  Pallas kernels  68.3 us (98%)
  local copies, waits for them, and re-layouts  1.57 us (2%)
    pallas_call x1, Pallas kernels, run(): pl.pallas_call(functools.partial(kernel, p), out_shape=jax.ShapeDtypeStru...  68.3 us
    unnamed x1, local copies, waits for them, and re-layouts  1.57 us

profile of v3, /device:TPU:0, one launch (start us, length us, event | category | flops | bytes accessed | tf_op | source)
XLA Modules:
  0.0 69.8 jit_solution(15833078361315566984)
XLA Ops:
  0.0 68.3 %chi.1 = f32[256,128]{1,0:T(8,128)} custom-call(s32[16]{0:T(128)} %index_in.1, f32[4096]{0:T(1024)} %energy_in.1, f32[8]{0:T(128)} %conduction_in.1, f32[4]{0:T(128)} %freq_in.1, bf16[2,24,9216]{2,1,0:T(8,128)(2,1)} %v_in.1, bf16[1,24,9216]{2,1,0:T(8,128)(2,1)} %c_in.1, s32[16,128]{1,0:T(8,128)} %bitcast.2, s32[1,4]{1,0:T(1,128)} %bitcast.3, ...), custom_call_target="tpu_custom_call" | custom-call | tf_op jit(solution)/shard_map/chi/pallas_call | solution.py:573
  68.3 1.6 %copy.15 = f32[256,128]{1,0:T(8,128)} copy(f32[256,128]{1,0:T(8,128)} %chi.1) | data formatting | bytes 262144

commit v4 on v3

--- a/solution.py
+++ b/solution.py
@@ -13,10 +13,10 @@
 LANE = 128
 SUB = 8
 INNER = 2
-STEPS = 6
+STEPS = 8
 UNROLL_PHASE = 4
 UNROLL_Y = 7
-UNROLL_Z = 2
+UNROLL_Z = 3
 MESH = pl.DeviceIdType.MESH
 VMEM_LIMIT = 66_000_000
 
@@ -71,7 +71,7 @@
     def stages(self):
         if self.merge > 1:
             return [list(range(self.chunks))]
-        return [list(range(k, min(k + 2, self.chunks))) for k in range(0, self.chunks, 2)]
+        return [list(range(min(2, self.chunks)))] + [[k] for k in range(2, self.chunks)]
 
     def arrivals(self, at):
         return sorted(range(self.outer), key=lambda o: (abs(o - at), o))
@@ -133,21 +133,29 @@
     return band // p.inner, lax.rem(band, p.inner)
 
 
+def wrap(a, n):
+    return jnp.where(a >= n, a - n, a)
+
+
 def remote(src, dst, send, recv, target):
     return pltpu.make_async_remote_copy(src, dst, send, recv, device_id=target, device_id_type=MESH)
 
 
 def kernel(p, index_in, energy_in, conduction_in, freq_in, v_in, c_in, cell_in, block_in, xt_in, *refs):
     n_win = len(p.windows())
+    zt_in = refs[:n_win]
+    yt_in, fold_in = refs[n_win : n_win + 2]
+    refs = refs[n_win + 2 :]
+    (chi_ref, *refs) = refs
     zt_refs = refs[:n_win]
-    (yt_ref, fold_ref, chi_ref, z_ref, planes_ref, pick_a, pick_b, v_ref, c_ref, cells, blocks_v, blocks, pidx_v, pidx, code_ref,
-     phase_ref, xt_ref, part_ref, row1, sum_ref, row_ref, block1, block_ref, own_sem, vs, vr, cs, cr, cell_sem, sem1, sem2, met) = refs[n_win:]
+    (yt_ref, fold_ref, index_ref, energy_ref, level_ref, freq_ref, z_ref, planes_ref, pick_a, pick_b, v_ref, c_ref, cells, blocks_v, blocks, pidx_v, pidx, code_ref,
+     phase_ref, xt_ref, part_ref, row1, sum_ref, row_ref, block1, block_ref, own_sem, vs, vr, cs, cr, cell_sem, sem1, sem2, met, table_sem) = refs[n_win:]
     f32, bf16, i32 = jnp.float32, jnp.bfloat16, jnp.int32
     outer, inner = place(p)
     col, band = lax.axis_index("col"), lax.axis_index("band")
     line = [(outer > 0, outer - 1), (outer < p.outer - 1, outer + 1)]
-    near = [(band, lax.rem(col + d, p.cols)) for d in range(1, p.cols)]
-    near += [(outer * p.inner + lax.rem(inner + d, p.inner), col) for d in range(1, p.inner)]
+    near = [(band, wrap(col + d, p.cols)) for d in range(1, p.cols)]
+    near += [(outer * p.inner + wrap(inner + d, p.inner), col) for d in range(1, p.inner)]
     greeted = len(near) + sum(jnp.where(there, 1, 0) for there, _ in line)
 
     barrier = pltpu.get_barrier_semaphore()
@@ -168,6 +176,11 @@
     ]
     for copy in local:
         copy.start()
+    tables = [*zip(zt_in, zt_refs), (yt_in, yt_ref), (fold_in, fold_ref), (index_in, index_ref)]
+    tables += [(energy_in, energy_ref), (conduction_in, level_ref), (freq_in, freq_ref)]
+    tables = [pltpu.make_async_copy(src, dst, table_sem.at[k]) for k, (src, dst) in enumerate(tables)]
+    for copy in tables:
+        copy.start()
     pl.semaphore_wait(barrier, greeted)
 
     step_lanes = p.gy * p.gz // p.steps
@@ -177,7 +190,7 @@
 
     def v_copy(d, step):
         slot = v_ref.at[pl.ds(inner * p.v_own, p.v_own)]
-        target = (outer * p.inner + lax.rem(inner + d, p.inner), col)
+        target = (outer * p.inner + wrap(inner + d, p.inner), col)
         return remote(cut(v_in, step), cut(slot, step), vs.at[d - 1, step], vr.at[d - 1, step], target)
 
     def hop(way, d, step):
@@ -215,7 +228,7 @@
 
     cell_copies = []
     for d in range(1, p.cols):
-        target = (band, lax.rem(col + d, p.cols))
+        target = (band, wrap(col + d, p.cols))
         cell_copies.append(remote(cell_in, cells.at[col], cell_sem.at[0, 0, d - 1], cell_sem.at[1, 0, d - 1], target))
         cell_copies.append(remote(block_in, blocks_v.at[col], cell_sem.at[0, 1, d - 1], cell_sem.at[1, 1, d - 1], target))
     for copy in cell_copies:
@@ -361,7 +374,7 @@
                 pass_on(d, step)
             if t == 0:
                 if step == 0:
-                    for copy in local[:2]:
+                    for copy in local[:2] + tables:
                         copy.wait()
                 for d in range(1, p.inner):
                     v_copy(d, step).wait_recv()
@@ -370,7 +383,7 @@
             looped(groups * step, groups * (step + 1), functools.partial(z_step, stage), UNROLL_Z)
         passed = until
     for d in range(1, p.inner):
-        target = (outer * p.inner + lax.rem(inner + d, p.inner), col)
+        target = (outer * p.inner + wrap(inner + d, p.inner), col)
         pl.semaphore_signal(met, inc=1, device_id=target, device_id_type=MESH)
     to_scalar.wait()
     looped(0, p.half, functools.partial(y_step, stages[-1]), UNROLL_Y)
@@ -379,11 +392,13 @@
 
     def target_band(t):
         back = p.bands - 1 - t
-        o = lax.rem(outer + lax.div(back, p.inner), p.outer)
-        return o * p.inner + lax.rem(inner + lax.rem(back, p.inner), p.inner)
+        high = (back * (65536 // p.inner + 1)) >> 16
+        return wrap(outer + high, p.outer) * p.inner + wrap(inner + back - high * p.inner, p.inner)
+
+    peers = [wrap(col + 1 + c, p.cols) for c in range(p.cols)]
 
     def number(t, c):
-        return lax.rem(col + 1 + c, p.cols) * p.bands + target_band(t)
+        return peers[c] * p.bands + target_band(t)
 
     def pick(d, buf):
         at = d * p.halves
@@ -409,7 +424,7 @@
         part_ref[d] = total.astype(bf16)
 
     def peer(c):
-        return (band, lax.rem(col + 1 + c, p.cols))
+        return (band, peers[c])
 
     def part_copy(t, c):
         return remote(part_ref.at[number(t, c)], row1.at[c, t], sem1.at[0, c, t], sem1.at[1, c, t], peer(c))
@@ -468,7 +483,7 @@
                 if c > 1:
                     part_copy(t, c - 2).start()
             if c == 1:
-                when(t > 1, lambda: send_sums(t - 2))
+                when(t > 2, lambda: send_sums(t - 3))
             if c == min(2, p.cols - 1):
 
                 @pl.when(t == 0)
@@ -480,16 +495,18 @@
         def _():
             sum_ref[p.bands, : p.block_rows, :] = add_up_block()
 
-        @pl.when(t > 0)
+        @pl.when(t > 1)
         def _():
-            sum_ref[t - 1] = add_up(t - 1)
+            sum_ref[t - 2] = add_up(t - 2)
 
         return carry
 
     lax.fori_loop(0, p.bands, walk, 0)
     last = p.bands - 1
     part_copy(last, p.cols - 2).start()
+    sum_ref[last - 1] = add_up(last - 1)
     turn(number(last, p.cols - 1), buffers[0])
+    send_sums(last - 2)
     send_sums(last - 1)
     row_ref[band] = add_up(last)
     block_ref[band] = sum_ref[p.bands, : p.block_rows, :]
@@ -531,10 +548,10 @@
             out = jnp.where(which == k, value, out)
         return out
 
-    valence = [energy_in[index_in[i]] for i in range(p.valences)]
+    valence = [energy_ref[index_ref[i]] for i in range(p.valences)]
     valence = [spread(pair_v, valence[o * p.nv : (o + 1) * p.nv]) for o in range(p.outer)]
     conduction = [
-        spread(pair_c, [conduction_in[(o * p.inner + i) * p.c_own + l] for o in range(p.outer) for l in range(p.c_own)])
+        spread(pair_c, [level_ref[(o * p.inner + i) * p.c_own + l] for o in range(p.outer) for l in range(p.c_own)])
         for i in range(p.inner)
     ]
     norm = 1.0 / math.sqrt(p.valences * p.conductions)
@@ -552,7 +569,7 @@
         gap = conduction[b % p.inner] - valence[b // p.inner]
         parts = []
         for w in range(p.freqs):
-            weight = -4.0 * gap / (gap * gap + freq_in[w] * freq_in[w]) * norm
+            weight = -4.0 * gap / (gap * gap + freq_ref[w] * freq_ref[w]) * norm
             parts += [weight * first, weight * turned]
         right = jnp.concatenate(parts, axis=0)
         for q in range(p.pack):
@@ -573,9 +590,11 @@
     return pl.pallas_call(
         functools.partial(kernel, p),
         out_shape=jax.ShapeDtypeStruct((p.rows_dest, 2 * p.freqs * p.blocks), f32),
-        in_specs=[pl.BlockSpec(memory_space=pltpu.SMEM)] * 4 + [hbm] * 5 + [vmem] * len(tables),
+        in_specs=[hbm] * (9 + len(tables)),
         out_specs=vmem,
-        scratch_shapes=[
+        scratch_shapes=[pltpu.VMEM(t.shape, bf16) for t in tables]
+        + [pltpu.SMEM(a.shape, a.dtype) for a in (index, energy, conduction, freq)]
+        + [
             pltpu.VMEM((p.chunks, (p.gy + 1) * p.zpitch, LANE), f32),
             pltpu.VMEM(((p.half * p.gy + 1) * p.pitch, LANE), f32),
             pltpu.VMEM(((p.rows_dest + 1) * p.pitch, LANE), f32),
@@ -605,6 +624,7 @@
             dma((2, p.cols - 1, p.bands + 1)),
             dma((2, 2, p.bands)),
             pltpu.SemaphoreType.REGULAR,
+            dma((len(tables) + 4,)),
         ],
         compiler_params=pltpu.CompilerParams(
             collective_id=0, has_side_effects=True, vmem_limit_bytes=VMEM_LIMIT

time: 70 us -> 68 us (0.971)
  Pallas kernels: 68.3 us -> 66.3 us
    pallas_call x1, Pallas kernels: 68.3 us -> 66.3 us  [run(): pl.pallas_call(functools.partial(kernel, p), out_shape=jax.ShapeDtypeStru...]
where the time goes in v4:
time: 68 us; the launch traced here: 67.9 us
  Pallas kernels  66.3 us (98%)
  local copies, waits for them, and re-layouts  1.57 us (2%)
    pallas_call x1, Pallas kernels, run(): pl.pallas_call(functools.partial(kernel, p), out_shape=jax.ShapeDtypeStru...  66.3 us
    unnamed x1, local copies, waits for them, and re-layouts  1.57 us

profile of v4, /device:TPU:0, one launch (start us, length us, event | category | flops | bytes accessed | tf_op | source)
XLA Modules:
  0.0 67.9 jit_solution(9277440953347339890)
XLA Ops:
  0.0 66.3 %chi.1 = f32[256,128]{1,0:T(8,128)} custom-call(s32[16]{0:T(128)} %index_in.1, f32[4096]{0:T(1024)} %energy_in.1, f32[8]{0:T(128)} %conduction_in.1, f32[4]{0:T(128)} %freq_in.1, bf16[2,24,9216]{2,1,0:T(8,128)(2,1)} %v_in.1, bf16[1,24,9216]{2,1,0:T(8,128)(2,1)} %c_in.1, s32[16,128]{1,0:T(8,128)} %bitcast.2, s32[1,4]{1,0:T(1,128)} %bitcast.3, ...), custom_call_target="tpu_custom_call" | custom-call | tf_op jit(solution)/shard_map/chi/pallas_call | solution.py:590
  66.3 1.6 %copy.15 = f32[256,128]{1,0:T(8,128)} copy(f32[256,128]{1,0:T(8,128)} %chi.1) | data formatting | bytes 262144

commit v5 on v4

--- a/solution.py
+++ b/solution.py
@@ -511,33 +511,6 @@
     row_ref[band] = add_up(last)
     block_ref[band] = sum_ref[p.bands, : p.block_rows, :]
 
-    for step in range(p.steps):
-        for d in range(p.outer - 1):
-            for way in range(2):
-
-                @pl.when(passes(way, d))
-                def _():
-                    hop(way, d, step).wait_send()
-
-        for d in range(1, p.inner):
-            v_copy(d, step).wait_send()
-
-    def close_parts(t, carry):
-        for c in range(p.cols - 1):
-            part_copy(t, c).wait_send()
-        return carry
-
-    lax.fori_loop(0, p.bands, close_parts, 0)
-    for c in range(p.cols - 1):
-        block_part_copy(c).wait_send()
-
-    def close_sums(t, carry):
-        for copy in sum_copies(t):
-            copy.wait()
-        return carry
-
-    lax.fori_loop(0, p.bands - 1, close_sums, 0)
-
     pair_lane = lax.broadcasted_iota(i32, (1, LANE), 1)
     pair = lax.rem(pair_lane, p.pairs)
     pair_v, pair_c = lax.rem(pair, p.nv), lax.div(pair, p.nv)
@@ -555,6 +528,38 @@
         for i in range(p.inner)
     ]
     norm = 1.0 / math.sqrt(p.valences * p.conductions)
+    weights = []
+    for b in range(p.bands):
+        gap = conduction[b % p.inner] - valence[b // p.inner]
+        weights.append([-4.0 * gap / (gap * gap + freq_ref[w] * freq_ref[w]) * norm for w in range(p.freqs)])
+
+    for step in range(p.steps):
+        for d in range(p.outer - 1):
+            for way in range(2):
+
+                @pl.when(passes(way, d))
+                def _():
+                    hop(way, d, step).wait_send()
+
+        for d in range(1, p.inner):
+            v_copy(d, step).wait_send()
+
+    def close_parts(t, carry):
+        for c in range(p.cols - 1):
+            part_copy(t, c).wait_send()
+        return carry
+
+    lax.fori_loop(0, p.bands, close_parts, 0)
+    for c in range(p.cols - 1):
+        block_part_copy(c).wait_send()
+
+    def close_sums(t, carry):
+        for copy in sum_copies(t):
+            copy.wait()
+        return carry
+
+    lax.fori_loop(0, p.bands - 1, close_sums, 0)
+
     group_lanes = 2 * p.pairs
     acc = [jnp.zeros((p.rows_packed, 2 * p.freqs * p.blocks), f32) for _ in range(p.pack)]
     for b in range(p.bands):
@@ -566,10 +571,9 @@
             -pltpu.roll(first, LANE - p.pairs, 1),
             jnp.where(pair_lane < group_lanes, pltpu.roll(first, p.pairs, 1), 0.0),
         )
-        gap = conduction[b % p.inner] - valence[b // p.inner]
         parts = []
         for w in range(p.freqs):
-            weight = -4.0 * gap / (gap * gap + freq_ref[w] * freq_ref[w]) * norm
+            weight = weights[b][w]
             parts += [weight * first, weight * turned]
         right = jnp.concatenate(parts, axis=0)
         for q in range(p.pack):

time: 68 us -> 68 us (level)
  no operation moved by 1% of the time
where the time goes in v5:
time: 68 us; the launch traced here: 67.9 us
  Pallas kernels  66.3 us (98%)
  local copies, waits for them, and re-layouts  1.57 us (2%)
    pallas_call x1, Pallas kernels, run(): pl.pallas_call(functools.partial(kernel, p), out_shape=jax.ShapeDtypeStru...  66.3 us
    unnamed x1, local copies, waits for them, and re-layouts  1.57 us

profile of v5, /device:TPU:0, one launch (start us, length us, event | category | flops | bytes accessed | tf_op | source)
XLA Modules:
  0.0 67.9 jit_solution(7565647329314828198)
XLA Ops:
  0.0 66.3 %chi.1 = f32[256,128]{1,0:T(8,128)} custom-call(s32[16]{0:T(128)} %index_in.1, f32[4096]{0:T(1024)} %energy_in.1, f32[8]{0:T(128)} %conduction_in.1, f32[4]{0:T(128)} %freq_in.1, bf16[2,24,9216]{2,1,0:T(8,128)(2,1)} %v_in.1, bf16[1,24,9216]{2,1,0:T(8,128)(2,1)} %c_in.1, s32[16,128]{1,0:T(8,128)} %bitcast.2, s32[1,4]{1,0:T(1,128)} %bitcast.3, ...), custom_call_target="tpu_custom_call" | custom-call | tf_op jit(solution)/shard_map/chi/pallas_call | solution.py:594
  66.3 1.6 %copy.15 = f32[256,128]{1,0:T(8,128)} copy(f32[256,128]{1,0:T(8,128)} %chi.1) | data formatting | bytes 262144
